TPU v7x, 128 devices: a whole 4x4x4 slice. The times are simulated.
128 devices in a mesh: row: 4 (over y), col: 32 (over z, x, core).
Axes of the slice: x: 4, y: 4, z: 4, core: 2. Of those that a mesh axis runs over, the one named last changes fastest.
Arguments:
- rhs: float32 [16384, 256], P(('row', 'col')), may hold values from -6 to 6
- dense: float32 [2, 16384, 16384], P(None, 'col', 'row'), may hold values from -0.03125 to 0.03125
- inflow: float32 [128, 2, 2, 512, 256], P(('row', 'col')), may hold values from -0.25 to 0.25
- robin: float32 [128, 2, 2, 512, 512], P(('row', 'col')), may hold values from -0.1875 to 0.1875
- outflow: float32 [128, 2, 256, 1024], P(('row', 'col')), may hold values from -0.0390625 to 0.0390625
- trace_row: int32 [32, 128, 8], replicated, may hold values from 0 to 511
- trace_count: int32 [32, 128], replicated, may hold values from 0 to 8, as said below
- current_row: int32 [128, 128, 2], replicated, may hold values from 0 to 127
- current_count: int32 [128, 128], replicated, may hold values from 0 to 2, as said below
Outputs:
- solution: float32 [16384, 256], P(('row', 'col'))
Inputs may be any that keep to these rules, and one draw needn't show every extreme that they name: `trace_row`: repeats may occur. `trace_count`: 8 is reached, and some subdomain takes 8 from every block. `current_row`: repeats may occur. `current_count`: some subdomain gives 2 to every block, and some block receives 2 from every subdomain.
All inputs are finite; a program needn't handle non-finite values.
Results may differ from a plain program's by a relative error of at most 0.0001.
Values sent between devices are 32-bit elements; how exact they have to be, the bound alone decides.
A program may use at most 128 MiB of HBM per device.

v0:
```python
import jax
import jax.numpy as jnp
from jax import lax
from jax.sharding import PartitionSpec as P

ITERS = 2


EPS = 1e-06
HIGH = lax.Precision.HIGHEST


def extended(x, sides, width):
    for axis, dim in sides:
        size, length = (lax.axis_size(axis), x.shape[dim])
        up = [(i, (i + 1) % size) for i in range(size - 1)]
        down = [(j, i) for i, j in up]
        last = lax.slice_in_dim(x, length - width, length, axis=dim)
        leading = lax.slice_in_dim(x, 0, width, axis=dim)
        before = lax.ppermute(last, axis, up)
        after = lax.ppermute(leading, axis, down)
        x = jnp.concatenate([before, x, after], axis=dim)
    return x


def combine(real_half, imag_half, waves):
    return jnp.concatenate(
        [
            real_half[..., :waves] - imag_half[..., waves:],
            real_half[..., waves:] + imag_half[..., :waves],
        ],
        axis=-1,
    )


def scale_vector(vector, coef, waves):
    real_part = vector[:, :waves]
    imag_part = vector[:, waves:]
    return jnp.concatenate(
        [coef[0] * real_part - coef[1] * imag_part, coef[0] * imag_part + coef[1] * real_part],
        axis=1,
    )


def inner_terms(left, right, waves):
    left_real, left_imag = (left[:, :waves], left[:, waves:])
    right_real, right_imag = (right[:, :waves], right[:, waves:])
    return (
        jnp.sum(left_real * right_real + left_imag * right_imag, axis=0),
        jnp.sum(left_real * right_imag - left_imag * right_real, axis=0),
    )


def square_terms(vector, waves):
    halves = jnp.sum(vector * vector, axis=0)
    return halves[:waves] + halves[waves:]


def cmul(first, second):
    return (
        first[0] * second[0] - first[1] * second[1],
        first[0] * second[1] + first[1] * second[0],
    )


def cconj(first):
    return (first[0], -first[1])


def csub(first, second):
    return (first[0] - second[0], first[1] - second[1])


def cadd(first, second):
    return (first[0] + second[0], first[1] + second[1])


def cdiv(first, second):
    denom = second[0] * second[0] + second[1] * second[1]
    numer = cmul(first, cconj(second))
    return (numer[0] / denom, numer[1] / denom)


def solve_small(gram, target):
    size = len(target)
    gram = [list(line) for line in gram]
    target = list(target)
    for pivot in range(size):
        for lower in range(pivot + 1, size):
            factor = cdiv(gram[lower][pivot], gram[pivot][pivot])
            for other in range(pivot, size):
                gram[lower][other] = csub(gram[lower][other], cmul(factor, gram[pivot][other]))
            target[lower] = csub(target[lower], cmul(factor, target[pivot]))
    result = [None] * size
    for pivot in reversed(range(size)):
        summed = target[pivot]
        for other in range(pivot + 1, size):
            summed = csub(summed, cmul(gram[pivot][other], result[other]))
        result[pivot] = cdiv(summed, gram[pivot][pivot])
    return result


def least_squares(hess, beta, steps):
    zero_pair = (jnp.zeros_like(beta), jnp.zeros_like(beta))
    gram = []
    for first in range(steps):
        line = []
        for second in range(steps):
            summed = zero_pair
            for height in range(steps + 1):
                summed = cadd(
                    summed,
                    cmul(
                        cconj(hess.get((height, first), zero_pair)),
                        hess.get((height, second), zero_pair),
                    ),
                )
            line.append(summed)
        gram.append(line)
    target = [
        cmul(cconj(hess.get((0, first), zero_pair)), (beta, jnp.zeros_like(beta)))
        for first in range(steps)
    ]
    return solve_small(gram, target)


def on_device(
    rhs, dense, inflow, robin, outflow, trace_row, trace_count, current_row, current_count
):
    n_row = lax.axis_size("row")
    n_col = lax.axis_size("col")
    devices = n_row * n_col
    row_at = lax.axis_index("row")
    col_at = lax.axis_index("col")
    device_at = row_at * n_col + col_at
    block_rows, lanes = rhs.shape
    waves = lanes // 2
    tpair = trace_row.shape[2]
    tback = current_row.shape[2]
    inflow_mine = inflow[0]
    robin_mine = robin[0]
    outflow_mine = outflow[0]
    trace_rows = lax.dynamic_index_in_dim(trace_row, col_at, 0, keepdims=False)
    trace_live = lax.dynamic_index_in_dim(trace_count, col_at, 0, keepdims=False)
    trace_keep = (jnp.arange(tpair, dtype=jnp.int32)[None, :] < trace_live[:, None]).astype(
        jnp.float32
    )

    def reduce_sums(parts):
        return lax.psum((parts[0], parts[1], parts[2]), ("row", "col"))

    zero_line = jnp.zeros((1, waves), jnp.float32)
    unused_real, unused_imag, norm_start = reduce_sums(
        (zero_line, zero_line, square_terms(rhs, waves))
    )
    beta = jnp.sqrt(norm_start + EPS)
    basis = [rhs / jnp.concatenate([beta, beta])[None, :]]
    hess = {}
    for step in range(ITERS):
        operate_vector = basis[step]
        piece = lax.all_gather(operate_vector, "col", axis=0, tiled=True)
        real_cols = dense[0]
        imag_cols = dense[1]
        real_half = jnp.dot(real_cols, piece, precision=HIGH, preferred_element_type=jnp.float32)
        imag_half = jnp.dot(imag_cols, piece, precision=HIGH, preferred_element_type=jnp.float32)
        buffer = (
            jnp.take(combine(real_half, imag_half, waves), trace_rows.reshape(-1), axis=0).reshape(
                devices, tpair, lanes
            )
            * trace_keep[:, :, None]
        )
        arrived = lax.all_to_all(buffer, ("row", "col"), split_axis=0, concat_axis=0, tiled=True)
        slots = jnp.sum(arrived.reshape(n_row, n_col, tpair, lanes), axis=0)
        slots = slots.reshape(n_col * tpair, lanes)
        mixed = jnp.einsum("fpmk,kl->fpml", inflow_mine, slots, precision=HIGH)
        excite = combine(mixed[:, 0], mixed[:, 1], waves)
        mixed = jnp.einsum("fpmn,fnl->fpml", robin_mine, excite, precision=HIGH)
        local = combine(mixed[:, 0], mixed[:, 1], waves)
        padded = extended(local, ((("row", "col"), 0),), 1)
        near = jnp.stack([padded[0], padded[3]], axis=0)
        mixed = jnp.einsum("fpmn,fnl->fpml", robin_mine, near, precision=HIGH)
        faces = local + combine(mixed[:, 0], mixed[:, 1], waves)
        flat = faces.reshape(faces.shape[0] * faces.shape[1], lanes)
        mixed = jnp.einsum("pkn,nl->pkl", outflow_mine, flat, precision=HIGH)
        currents = combine(mixed[0], mixed[1], waves)
        operate_arrived = lax.all_to_all(
            currents.reshape(devices, tback, lanes),
            ("row", "col"),
            split_axis=0,
            concat_axis=0,
            tiled=True,
        )
        own_rows = lax.dynamic_index_in_dim(current_row, device_at, 0, keepdims=False)
        own_live = lax.dynamic_index_in_dim(current_count, device_at, 0, keepdims=False)
        alive = (jnp.arange(tback, dtype=jnp.int32)[None, :] < own_live[:, None]).astype(
            jnp.float32
        )
        landed = (
            jnp.zeros((block_rows, lanes), jnp.float32)
            .at[own_rows.reshape(-1)]
            .add((operate_arrived * alive[..., None]).reshape(-1, lanes))
        )
        image = operate_vector + landed
        pairs = [inner_terms(basis[column], image, waves) for column in range(step + 1)]
        inner_real = jnp.stack([pair[0] for pair in pairs], axis=0)
        inner_imag = jnp.stack([pair[1] for pair in pairs], axis=0)
        inner_real, inner_imag, remain = reduce_sums(
            (inner_real, inner_imag, square_terms(image, waves))
        )
        for column in range(step + 1):
            coef = (inner_real[column], inner_imag[column])
            hess[column, step] = coef
            remain = remain - coef[0] * coef[0] - coef[1] * coef[1]
        height = jnp.sqrt(remain + EPS)
        hess[step + 1, step] = (height, jnp.zeros_like(height))
        if step + 1 < ITERS:
            update = image
            column = 0
            update = update - scale_vector(basis[column], hess[column, step], waves)
            basis.append(update / jnp.concatenate([height, height])[None, :])
    coeffs = least_squares(hess, beta, ITERS)
    solution = jnp.zeros_like(basis[0])
    for column in range(ITERS):
        solution = solution + scale_vector(basis[column], coeffs[column], waves)
    return solution


def solution(mesh):
    placed = (
        P(("row", "col"), None),
        P(None, "col", "row"),
        P(("row", "col"), None, None, None, None),
        P(("row", "col"), None, None, None, None),
        P(("row", "col"), None, None, None),
        P(),
        P(),
        P(),
        P(),
    )
    return jax.shard_map(
        on_device, mesh=mesh, in_specs=placed, out_specs=P(("row", "col"), None), check_vma=False
    )
```

profile of v0, /device:TPU:1, one launch (start us, length us, event | category | flops | bytes accessed | tf_op | source)
XLA Modules:
  0.0 568.6 jit_solution(6583387370913628874)
XLA Ops:
  7.6 68.7 %psum.49 = f32[128]{0:T(128)S(1)} all-reduce(f32[128]{0:T(128)S(1)} %slice_add_fusion.12), channel_id=1, replica_groups=mesh['row'=4,'col'=32] {'row','col'}, use_global_device_ids=true, to_apply=%region_1.2 | all-reduce | flops 128 | bytes 1024 | tf_op jit(solution)/shard_map/psum | solution.py:150
  79.6 41.4 %all-gather.3.cloned.1.call-done = f32[4096,256]{1,0:T(8,128)} async-done(((f32[128,256]{1,0:T(8,128)}), f32[4096,256]{1,0:T(8,128)}) %all-gather.3.cloned.1.call-update) | async-done | bytes 4194320 | tf_op jit(solution)/shard_map/all_gather | solution.py:161
  121.0 16.6 %fusion.52 = f32[512,256]{0,1:T(8,128)S(1)} fusion(f32[4096,256]{1,0:T(8,128)} %all-gather.3.cloned.1.call-done, f32[2,512,4096]{2,1,0:T(8,128)} %param.12), kind=kOutput, calls=%fused_computation.40 | convolution fusion | flops 6442450944 | bytes 13107200 | tf_op jit(solution)/shard_map/dot_general | solution.py:164
  137.7 16.6 %fusion.58 = f32[512,256]{0,1:T(8,128)S(1)} fusion(f32[4096,256]{1,0:T(8,128)S(1)} %copy-done.3, f32[2,512,4096]{2,1,0:T(8,128)} %param.12), kind=kOutput, calls=%fused_computation.42 | convolution fusion | flops 6442450944 | bytes 13107200 | tf_op jit(solution)/shard_map/dot_general | solution.py:165
  154.7 4.7 gather_fusion
  160.9 26.5 %all_to_all.20 = f32[128,8,256]{2,1,0:T(8,128)S(1)} all-to-all(f32[128,8,256]{2,1,0:T(8,128)S(1)} %bitcast_multiply_fusion.1), channel_id=1, replica_groups=mesh['row'=4,'col'=32] {'row','col'}, dimensions={0} | all-to-all | bytes 2097152 | tf_op jit(solution)/shard_map/all_to_all | solution.py:172
  193.2 3.8 fusion.28
  207.8 4.4 collective-permute-done.1
  212.2 6.8 %fusion.31 = f32[2,2,512,256]{2,3,1,0:T(8,128)S(1)} fusion(f32[1,2,2,512,512]{4,3,2,1,0:T(8,128)} %param.14, f32[1,512,256]{1,2,0:T(8,128)} %collective-permute-done.1, f32[1,512,256]{1,2,0:T(8,128)} %collective-permute-done), kind=kOutput, calls=%fused_computation.33 | convolution fusion | flops 3221487616 | bytes 7340032 | tf_op jit(solution)/shard_map/fpmn,fnl->fpml/dot_general | solution.py:181
  224.5 5.5 fusion.46
  231.2 11.1 %all-to-all-start.1 = ((f32[128,2,256]{2,1,0:T(2,128)}), f32[128,2,256]{2,1,0:T(2,128)S(1)}, u32[]{:S(2)}, u32[]{:S(2)}) async-start(f32[128,2,256]{2,1,0:T(2,128)} %reshape.146), calls=%async_computation.1 | async-start | bytes 524288 | tf_op jit(solution)/shard_map/all_to_all | solution.py:186
  243.1 10.2 %all-to-all-done.1 = f32[128,2,256]{2,1,0:T(2,128)S(1)} async-done(((f32[128,2,256]{2,1,0:T(2,128)}), f32[128,2,256]{2,1,0:T(2,128)S(1)}, u32[]{:S(2)}, u32[]{:S(2)}) %all-to-all-start.1) | async-done | bytes 262176 | tf_op jit(solution)/shard_map/all_to_all | solution.py:186
  255.8 63.1 %all-reduce.1 = (f32[128]{0:T(128)S(1)}, f32[128]{0:T(128)S(1)}, f32[128]{0:T(128)S(1)}) all-reduce(f32[128]{0:T(128)S(1)} %get-tuple-element.11, f32[128]{0:T(128)S(1)} %slice_add_fusion.11, f32[128]{0:T(128)S(1)} %get-tuple-element.10), channel_id=1, replica_groups=mesh['row'=4,'col'=32] {'row','col'}, use_global_device_ids=true, to_apply=%region_7.9 | all-reduce | flops 384 | bytes 3072 | tf_op jit(solution)/shard_map/psum | solution.py:150
  319.6 42.9 %all-gather.5.cloned.1.call-done = f32[4096,256]{1,0:T(8,128)} async-done(((f32[128,256]{1,0:T(8,128)}), f32[4096,256]{1,0:T(8,128)}) %all-gather.5.cloned.1.call-update) | async-done | bytes 4194320 | tf_op jit(solution)/shard_map/all_gather | solution.py:161
  362.6 16.6 %fusion.55 = f32[512,256]{0,1:T(8,128)S(1)} fusion(f32[4096,256]{1,0:T(8,128)} %all-gather.5.cloned.1.call-done, f32[2,512,4096]{2,1,0:T(8,128)} %param.12), kind=kOutput, calls=%fused_computation.41 | convolution fusion | flops 6442450944 | bytes 13107200 | tf_op jit(solution)/shard_map/dot_general | solution.py:164
  379.2 16.6 %fusion.61 = f32[512,256]{0,1:T(8,128)S(1)} fusion(f32[4096,256]{1,0:T(8,128)S(1)} %copy-done.4, f32[2,512,4096]{2,1,0:T(8,128)} %param.12), kind=kOutput, calls=%fused_computation.43 | convolution fusion | flops 6442450944 | bytes 13107200 | tf_op jit(solution)/shard_map/dot_general | solution.py:165
  396.2 4.7 gather_fusion.1
  402.4 26.6 %all_to_all.21 = f32[128,8,256]{2,1,0:T(8,128)} all-to-all(f32[128,8,256]{2,1,0:T(8,128)S(1)} %bitcast_multiply_fusion), channel_id=1, replica_groups=mesh['row'=4,'col'=32] {'row','col'}, dimensions={0} | all-to-all | bytes 2097152 | tf_op jit(solution)/shard_map/all_to_all | solution.py:172
  450.7 4.4 collective-permute-done.3
  455.1 6.6 %fusion.37 = f32[2,2,512,256]{2,3,1,0:T(8,128)S(1)} fusion(f32[1,2,2,512,512]{4,3,2,1,0:T(8,128)} %param.14, f32[1,512,256]{1,2,0:T(8,128)} %collective-permute-done.3, f32[1,512,256]{1,2,0:T(8,128)} %collective-permute-done.2), kind=kOutput, calls=%fused_computation.35 | convolution fusion | flops 3221487616 | bytes 7340032 | tf_op jit(solution)/shard_map/fpmn,fnl->fpml/dot_general | solution.py:181
  466.1 5.7 fusion.49
  472.8 11.1 %all-to-all-start.3 = ((f32[128,2,256]{2,1,0:T(2,128)}), f32[128,2,256]{2,1,0:T(2,128)S(1)}, u32[]{:S(2)}, u32[]{:S(2)}) async-start(f32[128,2,256]{2,1,0:T(2,128)} %reshape.151), calls=%async_computation.3 | async-start | bytes 524288 | tf_op jit(solution)/shard_map/all_to_all | solution.py:186
  484.0 11.0 %all-to-all-done.3 = f32[128,2,256]{2,1,0:T(2,128)S(1)} async-done(((f32[128,2,256]{2,1,0:T(2,128)}), f32[128,2,256]{2,1,0:T(2,128)S(1)}, u32[]{:S(2)}, u32[]{:S(2)}) %all-to-all-start.3) | async-done | bytes 262176 | tf_op jit(solution)/shard_map/all_to_all | solution.py:186
  497.5 62.9 %all-reduce = (f32[128]{0:T(128)S(1)}, f32[2,128]{1,0:T(2,128)S(1)}, f32[2,128]{1,0:T(2,128)S(1)}) all-reduce(f32[128]{0:T(128)S(1)} %slice_add_fusion.10, f32[2,128]{1,0:T(2,128)S(1)} %get-tuple-element.84, f32[2,128]{1,0:T(2,128)S(1)} %get-tuple-element.83), channel_id=1, replica_groups=mesh['row'=4,'col'=32] {'row','col'}, use_global_device_ids=true, to_apply=%region_19.21 | all-reduce | flops 640 | bytes 5120 | tf_op jit(solution)/shard_map/psum | solution.py:150
  (118 shorter events, 65.6 us)
Async XLA Ops:
  6.5 180.9 %copy-start = (f32[1,2,2,512,256]{4,3,2,1,0:T(8,128)S(1)}, f32[1,2,2,512,256]{4,3,2,1,0:T(8,128)}, u32[]{:S(2)}) copy-start(f32[1,2,2,512,256]{4,3,2,1,0:T(8,128)} %param.13) | copy-start | bytes 6291460
  6.5 114.5 %all-gather.3.cloned.1.call-start = ((), (), s32[]{:S(2)}) async-start(), calls=%async_computation.4 | async-start | bytes 4325376 | tf_op jit(solution)/shard_map/all_gather | solution.py:161
  121.0 16.6 %copy-start.3 = (f32[4096,256]{1,0:T(8,128)S(1)}, f32[4096,256]{1,0:T(8,128)}, u32[]{:S(2)}) copy-start(f32[4096,256]{1,0:T(8,128)} %all-gather.3.cloned.1.call-done) | copy-start | bytes 12582916
  191.0 2.2 copy-start.1
  198.4 9.4 %collective-permute-start = (f32[1,512,256]{1,2,0:T(8,128)}, f32[1,512,256]{1,2,0:T(8,128)}, u32[]{:S(2)}, u32[]{:S(2)}) collective-permute-start(f32[1,512,256]{1,2,0:T(8,128)} %get-tuple-element.62), channel_id=1, source_target_pairs={{0,1},{1,2},{2,3},{3,4},{4,5},{5,6},{6,7},{7,8},{8,9},{9,10},{10,1... | collective-permute-start | bytes 1572872 | tf_op jit(solution)/shard_map/ppermute | solution.py:20
  201.4 10.8 %collective-permute-start.1 = (f32[1,512,256]{1,2,0:T(8,128)}, f32[1,512,256]{1,2,0:T(8,128)}, u32[]{:S(2)}, u32[]{:S(2)}) collective-permute-start(f32[1,512,256]{1,2,0:T(8,128)} %get-tuple-element.63), channel_id=1, source_target_pairs={{1,0},{2,1},{3,2},{4,3},{5,4},{6,5},{7,6},{8,7},{9,8},{10,9},{11,1... | collective-permute-start | bytes 1572872 | tf_op jit(solution)/shard_map/ppermute | solution.py:21
  219.0 5.5 copy-start.7
  224.5 18.5 %copy-start.5 = (f32[128,256]{1,0:T(8,128)S(1)}, f32[128,256]{1,0:T(8,128)}, u32[]{:S(2)}) copy-start(f32[128,256]{1,0:T(8,128)} %broadcast_divide_fusion) | copy-start | bytes 393220
  231.2 22.1 %all-to-all-start.1 = ((f32[128,2,256]{2,1,0:T(2,128)}), f32[128,2,256]{2,1,0:T(2,128)S(1)}, u32[]{:S(2)}, u32[]{:S(2)}) async-start(f32[128,2,256]{2,1,0:T(2,128)} %reshape.146), calls=%async_computation.1 | async-start | bytes 524288 | tf_op jit(solution)/shard_map/all_to_all | solution.py:186
  242.3 120.3 %all-gather.5.cloned.1.call-start = ((), (), s32[]{:S(2)}) async-start(), calls=%async_computation.5 | async-start | bytes 4325376 | tf_op jit(solution)/shard_map/all_gather | solution.py:161
  362.6 16.6 %copy-start.4 = (f32[4096,256]{1,0:T(8,128)S(1)}, f32[4096,256]{1,0:T(8,128)}, u32[]{:S(2)}) copy-start(f32[4096,256]{1,0:T(8,128)} %all-gather.5.cloned.1.call-done) | copy-start | bytes 12582916
  433.9 2.2 copy-start.2
  441.3 9.4 %collective-permute-start.2 = (f32[1,512,256]{1,2,0:T(8,128)}, f32[1,512,256]{1,2,0:T(8,128)}, u32[]{:S(2)}, u32[]{:S(2)}) collective-permute-start(f32[1,512,256]{1,2,0:T(8,128)} %get-tuple-element.58), channel_id=1, source_target_pairs={{0,1},{1,2},{2,3},{3,4},{4,5},{5,6},{6,7},{7,8},{8,9},{9,10},{10,1... | collective-permute-start | bytes 1572872 | tf_op jit(solution)/shard_map/ppermute | solution.py:20
  444.3 10.8 %collective-permute-start.3 = (f32[1,512,256]{1,2,0:T(8,128)}, f32[1,512,256]{1,2,0:T(8,128)}, u32[]{:S(2)}, u32[]{:S(2)}) collective-permute-start(f32[1,512,256]{1,2,0:T(8,128)} %get-tuple-element.59), channel_id=1, source_target_pairs={{1,0},{2,1},{3,2},{4,3},{5,4},{6,5},{7,6},{8,7},{9,8},{10,9},{11,1... | collective-permute-start | bytes 1572872 | tf_op jit(solution)/shard_map/ppermute | solution.py:21
  461.8 4.3 copy-start.8
  466.1 17.9 %copy-start.6 = (f32[128,256]{1,0:T(8,128)S(1)}, f32[128,256]{1,0:T(8,128)}, u32[]{:S(2)}) copy-start(f32[128,256]{1,0:T(8,128)} %fusion.90) | copy-start | bytes 393220
  472.8 22.1 %all-to-all-start.3 = ((f32[128,2,256]{2,1,0:T(2,128)}), f32[128,2,256]{2,1,0:T(2,128)S(1)}, u32[]{:S(2)}, u32[]{:S(2)}) async-start(f32[128,2,256]{2,1,0:T(2,128)} %reshape.151), calls=%async_computation.3 | async-start | bytes 524288 | tf_op jit(solution)/shard_map/all_to_all | solution.py:186
Sparse Core Ops, SparseCore 0:
  78.1 42.9 all-gather.2
  319.8 42.7 all-gather.4
where the time goes:
time: 576 us; the launch traced here: 569 us
  blocking collectives  248 us (43%)
  waiting for transfers between devices  119 us (21%)
  matrix products  106 us (18%)
  starting transfers between devices  32.5 us (6%)
  local copies, waits for them, and re-layouts  30.3 us (5%)
  other arithmetic  19.1 us (3%)
  between operations  14.5 us (3%)
    psum x3, blocking collectives, reduce_sums(): return lax.psum((parts[0], parts[1], parts[2]), ('row', 'col'))  195 us
    all_gather x2, waiting for transfers between devices, on_device(): piece = lax.all_gather(operate_vector, 'col', axis=0, tiled=True)  84.3 us
    all_to_all x2, blocking collectives, on_device(): lax.all_to_all(buffer, ('row', 'col'), split_axis=0, concat_axis=0, tiled...  53.1 us
    dot_general x2, matrix products, on_device(): jnp.dot(imag_cols, piece, precision=HIGH, preferred_element_type=jnp.floa...  33.3 us
    dot_general x2, matrix products, on_device(): jnp.dot(real_cols, piece, precision=HIGH, preferred_element_type=jnp.floa...  33.2 us
    all_to_all x2, starting transfers between devices, on_device(): lax.all_to_all(currents.reshape(devices, tback, lanes), ('row', 'col'), s...  22.2 us
    all_to_all x2, waiting for transfers between devices, on_device(): lax.all_to_all(currents.reshape(devices, tback, lanes), ('row', 'col'), s...  21.2 us
    dot_general x2, matrix products, on_device(): mixed = jnp.einsum('fpmn,fnl->fpml', robin_mine, near, precision=HIGH)  13.5 us
  transfers between devices with their start and end apart: 8, of which 8 were waited for; matrix products, arithmetic and copies ran while one was open for 1% of the time, Pallas kernels for 0%

commit v1 on v0

--- a/solution.py
+++ b/solution.py
@@ -7,7 +7,8 @@
 
 
 EPS = 1e-06
-HIGH = lax.Precision.HIGHEST
+SCALE = 2.0**-24
+HIGH = lax.Precision.HIGH
 
 
 def extended(x, sides, width):
@@ -124,6 +125,57 @@
     return solve_small(gram, target)
 
 
+def turned(vector, waves):
+    return jnp.concatenate([-vector[..., waves:], vector[..., :waves]], axis=-1)
+
+
+def conj_mul(first, second):
+    return cmul(cconj(first), second)
+
+
+def krylov_coefficients(sums):
+    norm0, p_real, p_imag, norm1, t_real, t_imag, s_real, s_imag, norm2 = sums
+    zero = jnp.zeros_like(norm0)
+    beta2 = norm0 + EPS
+    beta = jnp.sqrt(beta2)
+    unit = norm0 / beta2
+    lack = EPS / beta2
+    p = (p_real / beta2, p_imag / beta2)
+    q = norm1 / beta2
+    back = 1.0 / SCALE
+    t = ((t_real / beta2) * back, (t_imag / beta2) * back)
+    s = ((s_real / beta2) * back, (s_imag / beta2) * back)
+    z = ((norm2 / beta2) * back) * back
+    p_abs = p[0] * p[0] + p[1] * p[1]
+    h00 = (unit + p[0], p[1])
+    h10 = jnp.sqrt(unit * lack + 2.0 * lack * p[0] + (q - p_abs) + EPS)
+    a = 1.0 / h10
+    g = (lack - p[0], -p[1])
+    g_abs = g[0] * g[0] + g[1] * g[1]
+    gp = cmul(g, p)
+    h01 = (
+        a * (lack * h00[0] + (t[0] + gp[0])),
+        a * (lack * h00[1] + (t[1] + gp[1])),
+    )
+    short = a * a * (lack * (1.0 - lack) * (unit + 2.0 * p[0]) + lack * p_abs + EPS)
+    length = 1.0 - short
+    gt = conj_mul(g, t)
+    m = (
+        a * a * (s[0] + g[0] * q + gt[0] + g_abs * p[0]),
+        a * a * (s[1] + g[1] * q + gt[1] + g_abs * p[1]),
+    )
+    spread = a * a * (z + 2.0 * conj_mul(g, s)[0] + g_abs * q)
+    h11 = (length + m[0], m[1])
+    remain = length * short + 2.0 * short * m[0] + (spread - m[0] * m[0] - m[1] * m[1])
+    remain = remain - h01[0] * h01[0] - h01[1] * h01[1]
+    h21 = jnp.sqrt(remain + EPS)
+    hess = {(0, 0): h00, (1, 0): (h10, zero), (0, 1): h01, (1, 1): h11, (2, 1): (h21, zero)}
+    y0, y1 = least_squares(hess, beta, ITERS)
+    ya = (y1[0] * a, y1[1] * a)
+    yg = cmul(ya, g)
+    return ((y0[0] + yg[0]) / beta, (y0[1] + yg[1]) / beta), (ya[0] / beta, ya[1] / beta)
+
+
 def on_device(
     rhs, dense, inflow, robin, outflow, trace_row, trace_count, current_row, current_count
 ):
@@ -146,25 +198,18 @@
         jnp.float32
     )
 
-    def reduce_sums(parts):
-        return lax.psum((parts[0], parts[1], parts[2]), ("row", "col"))
-
-    zero_line = jnp.zeros((1, waves), jnp.float32)
-    unused_real, unused_imag, norm_start = reduce_sums(
-        (zero_line, zero_line, square_terms(rhs, waves))
-    )
-    beta = jnp.sqrt(norm_start + EPS)
-    basis = [rhs / jnp.concatenate([beta, beta])[None, :]]
-    hess = {}
+    basis = [rhs]
     for step in range(ITERS):
-        operate_vector = basis[step]
+        operate_vector = basis[step] if step == 0 else basis[step] * SCALE
         piece = lax.all_gather(operate_vector, "col", axis=0, tiled=True)
         real_cols = dense[0]
         imag_cols = dense[1]
-        real_half = jnp.dot(real_cols, piece, precision=HIGH, preferred_element_type=jnp.float32)
-        imag_half = jnp.dot(imag_cols, piece, precision=HIGH, preferred_element_type=jnp.float32)
+        field = jnp.dot(real_cols, piece, precision=HIGH, preferred_element_type=jnp.float32)
+        field = field + jnp.dot(
+            imag_cols, turned(piece, waves), precision=HIGH, preferred_element_type=jnp.float32
+        )
         buffer = (
-            jnp.take(combine(real_half, imag_half, waves), trace_rows.reshape(-1), axis=0).reshape(
+            jnp.take(field, trace_rows.reshape(-1), axis=0).reshape(
                 devices, tpair, lanes
             )
             * trace_keep[:, :, None]
@@ -200,29 +245,13 @@
             .at[own_rows.reshape(-1)]
             .add((operate_arrived * alive[..., None]).reshape(-1, lanes))
         )
-        image = operate_vector + landed
-        pairs = [inner_terms(basis[column], image, waves) for column in range(step + 1)]
-        inner_real = jnp.stack([pair[0] for pair in pairs], axis=0)
-        inner_imag = jnp.stack([pair[1] for pair in pairs], axis=0)
-        inner_real, inner_imag, remain = reduce_sums(
-            (inner_real, inner_imag, square_terms(image, waves))
-        )
-        for column in range(step + 1):
-            coef = (inner_real[column], inner_imag[column])
-            hess[column, step] = coef
-            remain = remain - coef[0] * coef[0] - coef[1] * coef[1]
-        height = jnp.sqrt(remain + EPS)
-        hess[step + 1, step] = (height, jnp.zeros_like(height))
-        if step + 1 < ITERS:
-            update = image
-            column = 0
-            update = update - scale_vector(basis[column], hess[column, step], waves)
-            basis.append(update / jnp.concatenate([height, height])[None, :])
-    coeffs = least_squares(hess, beta, ITERS)
-    solution = jnp.zeros_like(basis[0])
-    for column in range(ITERS):
-        solution = solution + scale_vector(basis[column], coeffs[column], waves)
-    return solution
+        basis.append(landed)
+    u0, b0, b1 = basis
+    sums = [square_terms(u0, waves), *inner_terms(u0, b0, waves), square_terms(b0, waves)]
+    sums += [*inner_terms(u0, b1, waves), *inner_terms(b0, b1, waves), square_terms(b1, waves)]
+    sums = lax.psum(jnp.stack(sums, axis=0), ("row", "col"))
+    first, second = krylov_coefficients([sums[i] for i in range(9)])
+    return scale_vector(u0, first, waves) + scale_vector(b0, second, waves)
 
 
 def solution(mesh):

time: 576 us -> 406 us (0.70)
  blocking collectives: 248 us -> 116 us
  matrix products: 106 us -> 58 us
  waiting for transfers between devices: 119 us -> 129 us
    psum x3 -> x1, blocking collectives: 195 us -> 63 us  [on_device(): sums = lax.psum(jnp.stack(sums, axis=0), ('row', 'col'))]
    dot_general x2, matrix products: 33.3 us -> 13.2 us  [on_device(): jnp.dot(imag_cols, turned(piece, waves), precision=HIGH, preferred_elemen...]
    dot_general x2, matrix products: 33.2 us -> 19.3 us  [on_device(): jnp.dot(real_cols, piece, precision=HIGH, preferred_element_type=jnp.floa...]
    all_gather x2, waiting for transfers between devices: 84.3 us -> 93.3 us  [on_device(): piece = lax.all_gather(operate_vector, 'col', axis=0, tiled=True)]
where the time goes in v1:
time: 406 us; the launch traced here: 399 us
  waiting for transfers between devices  129 us (32%)
  blocking collectives  116 us (29%)
  matrix products  58 us (14%)
  starting transfers between devices  33 us (8%)
  local copies, waits for them, and re-layouts  30.6 us (8%)
  other arithmetic  18.5 us (5%)
  between operations  14.2 us (3%)
    all_gather x2, waiting for transfers between devices, on_device(): piece = lax.all_gather(operate_vector, 'col', axis=0, tiled=True)  93.3 us
    psum x1, blocking collectives, on_device(): sums = lax.psum(jnp.stack(sums, axis=0), ('row', 'col'))  63 us
    all_to_all x2, blocking collectives, on_device(): lax.all_to_all(buffer, ('row', 'col'), split_axis=0, concat_axis=0, tiled...  53.2 us
    all_to_all x2, starting transfers between devices, on_device(): lax.all_to_all(currents.reshape(devices, tback, lanes), ('row', 'col'), s...  22.6 us
    all_to_all x2, waiting for transfers between devices, on_device(): lax.all_to_all(currents.reshape(devices, tback, lanes), ('row', 'col'), s...  20.8 us
    dot_general x2, matrix products, on_device(): jnp.dot(real_cols, piece, precision=HIGH, preferred_element_type=jnp.floa...  19.3 us
    dot_general x2, matrix products, on_device(): jnp.dot(imag_cols, turned(piece, waves), precision=HIGH, preferred_elemen...  13.2 us
    gather x2, local copies, waits for them, and re-layouts, on_device(): jnp.take(field, trace_rows.reshape(-1), axis=0)  9.36 us
  transfers between devices with their start and end apart: 8, of which 8 were waited for; matrix products, arithmetic and copies ran while one was open for 1% of the time, Pallas kernels for 0%

profile of v1, /device:TPU:1, one launch (start us, length us, event | category | flops | bytes accessed | tf_op | source)
XLA Modules:
  0.0 399.5 jit_solution(4154344122775271763)
XLA Ops:
  9.0 50.4 %all-gather.3.cloned.1.call-done = f32[4096,256]{1,0:T(8,128)} async-done(((f32[128,256]{1,0:T(8,128)}), f32[4096,256]{1,0:T(8,128)}) %all-gather.3.cloned.1.call-update) | async-done | bytes 4194320 | tf_op jit(solution)/shard_map/all_gather | solution.py:204
  62.0 7.8 %fusion.6 = f32[512,256]{1,0:T(8,128)S(1)} fusion(f32[4096,256]{1,0:T(8,128)} %all-gather.3.cloned.1.call-done, f32[2,512,4096]{2,1,0:T(8,128)} %param.12), kind=kOutput, calls=%fused_computation.10 | convolution fusion | flops 3221225472 | bytes 13107200 | tf_op jit(solution)/shard_map/dot_general | solution.py:207
  70.1 3.6 fusion.63
  73.7 4.7 %gather_fusion = f32[1024,256]{1,0:T(8,128)} fusion(f32[512,256]{1,0:T(8,128)S(1)} %fusion.63, s32[1024]{0:T(1024)S(1)} %fusion.110), kind=kCustom, calls=%fused_computation.clone | custom fusion | bytes 2101248 | tf_op jit(solution)/shard_map/jit(_take)/gather | solution.py:212
  79.9 26.8 %all_to_all.20 = f32[128,8,256]{2,1,0:T(8,128)S(1)} all-to-all(f32[128,8,256]{2,1,0:T(8,128)S(1)} %bitcast_multiply_fusion.1), channel_id=1, replica_groups=mesh['row'=4,'col'=32] {'row','col'}, dimensions={0} | all-to-all | bytes 2097152 | tf_op jit(solution)/shard_map/all_to_all | solution.py:217
  114.5 3.0 collective-permute-start
  124.0 4.4 %collective-permute-done.1 = f32[1,512,256]{1,2,0:T(8,128)} collective-permute-done((f32[1,512,256]{1,2,0:T(8,128)}, f32[1,512,256]{1,2,0:T(8,128)}, u32[]{:S(2)}, u32[]{:S(2)}) %collective-permute-start.1) | collective-permute-done | bytes 524320 | tf_op jit(solution)/shard_map/ppermute | solution.py:22
  128.4 4.4 %fusion.37 = f32[2,2,512,256]{2,3,1,0:T(8,128)S(1)} fusion(f32[1,2,2,512,512]{4,3,2,1,0:T(8,128)} %param.14, f32[1,512,256]{1,2,0:T(8,128)} %collective-permute-done.1, f32[1,512,256]{1,2,0:T(8,128)} %collective-permute-done), kind=kOutput, calls=%fused_computation.41 | convolution fusion | flops 1610874880 | bytes 7340032 | tf_op jit(solution)/shard_map/fpmn,fnl->fpml/dot_general | solution.py:226
  138.3 3.8 fusion.52
  143.2 11.1 %all-to-all-start.1 = ((f32[128,2,256]{2,1,0:T(2,128)}), f32[128,2,256]{2,1,0:T(2,128)S(1)}, u32[]{:S(2)}, u32[]{:S(2)}) async-start(f32[128,2,256]{2,1,0:T(2,128)} %reshape.140), calls=%async_computation.1 | async-start | bytes 524288 | tf_op jit(solution)/shard_map/all_to_all | solution.py:231
  155.3 10.0 %all-to-all-done.1 = f32[128,2,256]{2,1,0:T(2,128)S(1)} async-done(((f32[128,2,256]{2,1,0:T(2,128)}), f32[128,2,256]{2,1,0:T(2,128)S(1)}, u32[]{:S(2)}, u32[]{:S(2)}) %all-to-all-start.1) | async-done | bytes 262176 | tf_op jit(solution)/shard_map/all_to_all | solution.py:231
  168.4 42.9 %all-gather.5.cloned.1.call-done = f32[4096,256]{1,0:T(8,128)} async-done(((f32[128,256]{1,0:T(8,128)}), f32[4096,256]{1,0:T(8,128)}) %all-gather.5.cloned.1.call-update) | async-done | bytes 4194320 | tf_op jit(solution)/shard_map/all_gather | solution.py:204
  211.3 11.5 %fusion.4 = f32[256,512]{1,0:T(8,128)S(1)} fusion(f32[4096,256]{1,0:T(8,128)} %all-gather.5.cloned.1.call-done, f32[2,512,4096]{2,1,0:T(8,128)} %param.12), kind=kOutput, calls=%fused_computation.8 | convolution fusion | flops 3221225472 | bytes 13107200 | tf_op jit(solution)/shard_map/dot_general | solution.py:207
  223.1 9.6 %fusion.73 = f32[512,256]{0,1:T(8,128)S(1)} fusion(f32[256,512]{1,0:T(8,128)S(1)} %fusion.4, f32[2,512,4096]{2,1,0:T(8,128)} %param.12, f32[4096,128]{1,0:T(8,128)S(1)} %get-tuple-element.44, f32[4096,128]{1,0:T(8,128)S(1)} %get-tuple-element.43), kind=kOutput, calls=%fused_computation.51 | convolution fusion | flops 3222405120 | bytes 13631488 | tf_op jit(solution)/shard_map/dot_general | solution.py:208
  232.8 4.7 %gather_fusion.1 = f32[1024,256]{1,0:T(8,128)} fusion(f32[512,256]{1,0:T(8,128)S(1)} %copy.33, s32[1024]{0:T(1024)S(1)} %fusion.110), kind=kCustom, calls=%fused_computation.1.clone | custom fusion | bytes 2101248 | tf_op jit(solution)/shard_map/jit(_take)/gather | solution.py:212
  239.1 26.5 %all_to_all.21 = f32[128,8,256]{2,1,0:T(8,128)S(1)} all-to-all(f32[128,8,256]{2,1,0:T(8,128)S(1)} %bitcast_multiply_fusion), channel_id=1, replica_groups=mesh['row'=4,'col'=32] {'row','col'}, dimensions={0} | all-to-all | bytes 2097152 | tf_op jit(solution)/shard_map/all_to_all | solution.py:217
  275.0 3.0 collective-permute-start.2
  281.4 3.1 collective-permute-done.2
  284.4 4.4 %collective-permute-done.3 = f32[1,512,256]{1,2,0:T(8,128)} collective-permute-done((f32[1,512,256]{1,2,0:T(8,128)}, f32[1,512,256]{1,2,0:T(8,128)}, u32[]{:S(2)}, u32[]{:S(2)}) %collective-permute-start.3) | collective-permute-done | bytes 524320 | tf_op jit(solution)/shard_map/ppermute | solution.py:22
  288.8 4.4 %fusion.43 = f32[2,2,512,256]{2,3,1,0:T(8,128)S(1)} fusion(f32[1,2,2,512,512]{4,3,2,1,0:T(8,128)} %param.14, f32[1,512,256]{1,2,0:T(8,128)} %collective-permute-done.3, f32[1,512,256]{1,2,0:T(8,128)} %collective-permute-done.2), kind=kOutput, calls=%fused_computation.43 | convolution fusion | flops 1610874880 | bytes 7340032 | tf_op jit(solution)/shard_map/fpmn,fnl->fpml/dot_general | solution.py:226
  298.8 3.8 fusion.55
  303.6 11.5 %all-to-all-start.3 = ((f32[128,2,256]{2,1,0:T(2,128)}), f32[128,2,256]{2,1,0:T(2,128)S(1)}, u32[]{:S(2)}, u32[]{:S(2)}) async-start(f32[128,2,256]{2,1,0:T(2,128)} %reshape.145), calls=%async_computation.3 | async-start | bytes 524288 | tf_op jit(solution)/shard_map/all_to_all | solution.py:231
  315.1 10.8 %all-to-all-done.3 = f32[128,2,256]{2,1,0:T(2,128)S(1)} async-done(((f32[128,2,256]{2,1,0:T(2,128)}), f32[128,2,256]{2,1,0:T(2,128)S(1)}, u32[]{:S(2)}, u32[]{:S(2)}) %all-to-all-start.3) | async-done | bytes 262176 | tf_op jit(solution)/shard_map/all_to_all | solution.py:231
  328.5 63.0 %psum.7 = f32[9,128]{1,0:T(8,128)S(1)} all-reduce(f32[9,128]{1,0:T(8,128)S(1)} %stack.47), channel_id=1, replica_groups=mesh['row'=4,'col'=32] {'row','col'}, use_global_device_ids=true, to_apply=%region_13.15 | all-reduce | flops 1152 | bytes 9216 | tf_op jit(solution)/shard_map/psum | solution.py:252
  (100 shorter events, 56.1 us)
Async XLA Ops:
  6.5 100.3 %copy-start = (f32[1,2,2,512,256]{4,3,2,1,0:T(8,128)S(1)}, f32[1,2,2,512,256]{4,3,2,1,0:T(8,128)}, u32[]{:S(2)}) copy-start(f32[1,2,2,512,256]{4,3,2,1,0:T(8,128)} %param.13) | copy-start | bytes 6291460
  6.5 52.8 %all-gather.3.cloned.1.call-start = ((), (), s32[]{:S(2)}) async-start(), calls=%async_computation.4 | async-start | bytes 4325376 | tf_op jit(solution)/shard_map/all_gather | solution.py:204
  59.4 10.7 %copy-start.3 = (f32[2,512,4096]{2,1,0:T(8,128)S(1)}, f32[2,512,4096]{2,1,0:T(8,128)}, u32[]{:S(2)}) copy-start(f32[2,512,4096]{2,1,0:T(8,128)} %param.12) | copy-start | bytes 50331652
  108.7 2.2 copy-start.1
  114.5 9.4 %collective-permute-start = (f32[1,512,256]{1,2,0:T(8,128)}, f32[1,512,256]{1,2,0:T(8,128)}, u32[]{:S(2)}, u32[]{:S(2)}) collective-permute-start(f32[1,512,256]{1,2,0:T(8,128)} %get-tuple-element.73), channel_id=1, source_target_pairs={{0,1},{1,2},{2,3},{3,4},{4,5},{5,6},{6,7},{7,8},{8,9},{9,10},{10,1... | collective-permute-start | bytes 1572872 | tf_op jit(solution)/shard_map/ppermute | solution.py:21
  117.5 10.8 %collective-permute-start.1 = (f32[1,512,256]{1,2,0:T(8,128)}, f32[1,512,256]{1,2,0:T(8,128)}, u32[]{:S(2)}, u32[]{:S(2)}) collective-permute-start(f32[1,512,256]{1,2,0:T(8,128)} %get-tuple-element.74), channel_id=1, source_target_pairs={{1,0},{2,1},{3,2},{4,3},{5,4},{6,5},{7,6},{8,7},{9,8},{10,9},{11,1... | collective-permute-start | bytes 1572872 | tf_op jit(solution)/shard_map/ppermute | solution.py:22
  133.0 5.3 %copy-start.5 = (f32[2,512,128]{2,1,0:T(8,128)S(1)}, f32[2,512,128]{2,1,0:T(8,128)}, u32[]{:S(2)}) copy-start(f32[2,512,128]{2,1,0:T(8,128)} %copy.26) | copy-start | bytes 1572868
  143.2 22.1 %all-to-all-start.1 = ((f32[128,2,256]{2,1,0:T(2,128)}), f32[128,2,256]{2,1,0:T(2,128)S(1)}, u32[]{:S(2)}, u32[]{:S(2)}) async-start(f32[128,2,256]{2,1,0:T(2,128)} %reshape.140), calls=%async_computation.1 | async-start | bytes 524288 | tf_op jit(solution)/shard_map/all_to_all | solution.py:231
  154.3 57.0 %all-gather.5.cloned.1.call-start = ((), (), s32[]{:S(2)}) async-start(), calls=%async_computation.5 | async-start | bytes 4325376 | tf_op jit(solution)/shard_map/all_gather | solution.py:204
  211.3 11.5 %copy-start.4 = (f32[4096,256]{1,0:T(8,128)S(1)}, f32[4096,256]{1,0:T(8,128)}, u32[]{:S(2)}) copy-start(f32[4096,256]{1,0:T(8,128)} %all-gather.5.cloned.1.call-done) | copy-start | bytes 12582916
  269.1 2.2 copy-start.2
  273.7 6.4 %copy-start.7 = (f32[128,256]{1,0:T(8,128)S(1)}, f32[128,256]{1,0:T(8,128)}, u32[]{:S(2)}) copy-start(f32[128,256]{1,0:T(8,128)} %param.11) | copy-start | bytes 393220
  275.0 9.4 %collective-permute-start.2 = (f32[1,512,256]{1,2,0:T(8,128)}, f32[1,512,256]{1,2,0:T(8,128)}, u32[]{:S(2)}, u32[]{:S(2)}) collective-permute-start(f32[1,512,256]{1,2,0:T(8,128)} %get-tuple-element.71), channel_id=1, source_target_pairs={{0,1},{1,2},{2,3},{3,4},{4,5},{5,6},{6,7},{7,8},{8,9},{9,10},{10,1... | collective-permute-start | bytes 1572872 | tf_op jit(solution)/shard_map/ppermute | solution.py:21
  278.0 10.8 %collective-permute-start.3 = (f32[1,512,256]{1,2,0:T(8,128)}, f32[1,512,256]{1,2,0:T(8,128)}, u32[]{:S(2)}, u32[]{:S(2)}) collective-permute-start(f32[1,512,256]{1,2,0:T(8,128)} %get-tuple-element.72), channel_id=1, source_target_pairs={{1,0},{2,1},{3,2},{4,3},{5,4},{6,5},{7,6},{8,7},{9,8},{10,9},{11,1... | collective-permute-start | bytes 1572872 | tf_op jit(solution)/shard_map/ppermute | solution.py:22
  293.4 5.3 %copy-start.6 = (f32[2,512,128]{2,1,0:T(8,128)S(1)}, f32[2,512,128]{2,1,0:T(8,128)}, u32[]{:S(2)}) copy-start(f32[2,512,128]{2,1,0:T(8,128)} %copy.37) | copy-start | bytes 1572868
  303.6 22.3 %all-to-all-start.3 = ((f32[128,2,256]{2,1,0:T(2,128)}), f32[128,2,256]{2,1,0:T(2,128)S(1)}, u32[]{:S(2)}, u32[]{:S(2)}) async-start(f32[128,2,256]{2,1,0:T(2,128)} %reshape.145), calls=%async_computation.3 | async-start | bytes 524288 | tf_op jit(solution)/shard_map/all_to_all | solution.py:231
Sparse Core Ops, SparseCore 0:
  9.6 49.7 all-gather.2
  168.5 42.7 all-gather.4

commit v2 on v1

v2 whole, which is shorter than its diff:
```python
import functools

import jax
import jax.numpy as jnp
from jax import lax
from jax.experimental import pallas as pl
from jax.experimental.pallas import tpu as pltpu
from jax.sharding import PartitionSpec as P

ITERS = 2


EPS = 1e-06
SCALE = 2.0**-24
MESH = pl.DeviceIdType.MESH


def scale_vector(vector, coef, waves):
    real_part = vector[:, :waves]
    imag_part = vector[:, waves:]
    return jnp.concatenate(
        [coef[0] * real_part - coef[1] * imag_part, coef[0] * imag_part + coef[1] * real_part],
        axis=1,
    )


def inner_terms(left, right, waves):
    left_real, left_imag = (left[:, :waves], left[:, waves:])
    right_real, right_imag = (right[:, :waves], right[:, waves:])
    return (
        jnp.sum(left_real * right_real + left_imag * right_imag, axis=0),
        jnp.sum(left_real * right_imag - left_imag * right_real, axis=0),
    )


def square_terms(vector, waves):
    halves = jnp.sum(vector * vector, axis=0)
    return halves[:waves] + halves[waves:]


def cmul(first, second):
    return (
        first[0] * second[0] - first[1] * second[1],
        first[0] * second[1] + first[1] * second[0],
    )


def cconj(first):
    return (first[0], -first[1])


def csub(first, second):
    return (first[0] - second[0], first[1] - second[1])


def cadd(first, second):
    return (first[0] + second[0], first[1] + second[1])


def cdiv(first, second):
    denom = second[0] * second[0] + second[1] * second[1]
    numer = cmul(first, cconj(second))
    return (numer[0] / denom, numer[1] / denom)


def solve_small(gram, target):
    size = len(target)
    gram = [list(line) for line in gram]
    target = list(target)
    for pivot in range(size):
        for lower in range(pivot + 1, size):
            factor = cdiv(gram[lower][pivot], gram[pivot][pivot])
            for other in range(pivot, size):
                gram[lower][other] = csub(gram[lower][other], cmul(factor, gram[pivot][other]))
            target[lower] = csub(target[lower], cmul(factor, target[pivot]))
    result = [None] * size
    for pivot in reversed(range(size)):
        summed = target[pivot]
        for other in range(pivot + 1, size):
            summed = csub(summed, cmul(gram[pivot][other], result[other]))
        result[pivot] = cdiv(summed, gram[pivot][pivot])
    return result


def least_squares(hess, beta, steps):
    zero_pair = (jnp.zeros_like(beta), jnp.zeros_like(beta))
    gram = []
    for first in range(steps):
        line = []
        for second in range(steps):
            summed = zero_pair
            for height in range(steps + 1):
                summed = cadd(
                    summed,
                    cmul(
                        cconj(hess.get((height, first), zero_pair)),
                        hess.get((height, second), zero_pair),
                    ),
                )
            line.append(summed)
        gram.append(line)
    target = [
        cmul(cconj(hess.get((0, first), zero_pair)), (beta, jnp.zeros_like(beta)))
        for first in range(steps)
    ]
    return solve_small(gram, target)


def turned(vector):
    waves = vector.shape[-1] // 2
    return jnp.concatenate([-vector[..., waves:], vector[..., :waves]], axis=-1)


def conj_mul(first, second):
    return cmul(cconj(first), second)


def krylov_coefficients(sums):
    norm0, p_real, p_imag, norm1, t_real, t_imag, s_real, s_imag, norm2 = sums
    zero = jnp.zeros_like(norm0)
    beta2 = norm0 + EPS
    beta = jnp.sqrt(beta2)
    unit = norm0 / beta2
    lack = EPS / beta2
    p = (p_real / beta2, p_imag / beta2)
    q = norm1 / beta2
    back = 1.0 / SCALE
    t = ((t_real / beta2) * back, (t_imag / beta2) * back)
    s = ((s_real / beta2) * back, (s_imag / beta2) * back)
    z = ((norm2 / beta2) * back) * back
    p_abs = p[0] * p[0] + p[1] * p[1]
    h00 = (unit + p[0], p[1])
    h10 = jnp.sqrt(unit * lack + 2.0 * lack * p[0] + (q - p_abs) + EPS)
    a = 1.0 / h10
    g = (lack - p[0], -p[1])
    g_abs = g[0] * g[0] + g[1] * g[1]
    gp = cmul(g, p)
    h01 = (
        a * (lack * h00[0] + (t[0] + gp[0])),
        a * (lack * h00[1] + (t[1] + gp[1])),
    )
    short = a * a * (lack * (1.0 - lack) * (unit + 2.0 * p[0]) + lack * p_abs + EPS)
    length = 1.0 - short
    gt = conj_mul(g, t)
    m = (
        a * a * (s[0] + g[0] * q + gt[0] + g_abs * p[0]),
        a * a * (s[1] + g[1] * q + gt[1] + g_abs * p[1]),
    )
    spread = a * a * (z + 2.0 * conj_mul(g, s)[0] + g_abs * q)
    h11 = (length + m[0], m[1])
    remain = length * short + 2.0 * short * m[0] + (spread - m[0] * m[0] - m[1] * m[1])
    remain = remain - h01[0] * h01[0] - h01[1] * h01[1]
    h21 = jnp.sqrt(remain + EPS)
    hess = {(0, 0): h00, (1, 0): (h10, zero), (0, 1): h01, (1, 1): h11, (2, 1): (h21, zero)}
    y0, y1 = least_squares(hess, beta, ITERS)
    ya = (y1[0] * a, y1[1] * a)
    yg = cmul(ya, g)
    return ((y0[0] + yg[0]) / beta, (y0[1] + yg[1]) / beta), (ya[0] / beta, ya[1] / beta)


def split(x):
    high = x.astype(jnp.bfloat16)
    return high, (x - high.astype(jnp.float32)).astype(jnp.bfloat16)


def mm(a, b):
    return jnp.dot(a, b, preferred_element_type=jnp.float32)


def dot3(a, b):
    a_high, a_low = split(a)
    b_high, b_low = split(b)
    return mm(a_high, b_high) + (mm(a_high, b_low) + mm(a_low, b_high))


def pick(onehot, x):
    high, low = split(x)
    return mm(onehot, high) + mm(onehot, low)


def stacked(x):
    return jnp.concatenate([x, turned(x)], axis=0)


EVENTS = [
    (0, 0), (-1, 0), (1, 0), (0, -1), (0, 1), (2, 0), (-1, -1), (-1, 1),
    (1, -1), (1, 1), (0, 2), (2, -1), (2, 1), (-1, 2), (1, 2), (2, 2),
]


def kernel(
    n_row, n_col,
    rhs_hbm, dense_hbm, inflow_hbm, robin_hbm, outflow_hbm, tid_ref, sid_ref,
    out_ref,
    vfull, dstage, acc, gmat, gbuf, ybuf, sbuf, slots, infl, rob, outf,
    rin, orob, town, faces, nbuf, cur, curh, zbuf, zz, fin, basis, gram, gy, gram2, gc,
    load_sem, dsem, ag_send, ag_recv, y_send, y_recv, c_send, c_recv,
    f_send, f_recv, z_send, z_recv, e_send, e_recv, gy_send, gy_recv, gc_send, gc_recv,
):
    row = lax.axis_index("row")
    col = lax.axis_index("col")
    device = row * n_col + col
    total = n_row * n_col
    up = lax.rem(device + 1, total)
    down = lax.rem(device + total - 1, total)
    z = col // 8
    x = lax.rem(col // 2, 4)
    core = lax.rem(col, 2)
    stride_a = 8 - 6 * core
    stride_b = 2 + 6 * core
    at_a = z * (1 - core) + x * core
    at_b = x * (1 - core) + z * core

    def mine(da, db):
        return lax.rem(at_a + (da + 4), 4) * stride_a + lax.rem(at_b + (db + 4), 4) * stride_b + core

    def theirs(da, db):
        return (
            lax.rem(at_b + (da + 4), 4) * stride_b
            + lax.rem(at_a + (db + 4), 4) * stride_a
            + (1 - core)
        )

    partner = col + 1 - 2 * core
    half_rows = vfull.shape[1] // 2

    loads = [
        pltpu.make_async_copy(rhs_hbm, vfull.at[col], load_sem.at[0]),
        pltpu.make_async_copy(rhs_hbm, basis.at[0], load_sem.at[1]),
    ]
    for copy in loads:
        copy.start()

    def dense_copy(part, index):
        return pltpu.make_async_copy(
            dense_hbm.at[part, :, pl.ds(pl.multiple_of(index * 128, 128), 128)],
            dstage.at[index, :, pl.ds(part * 128, 128)],
            dsem.at[part, index],
        )

    @pl.loop(0, n_col)
    def _(k):
        index = lax.rem(col + k, n_col)
        dense_copy(0, index).start()
        dense_copy(1, index).start()

    small = []
    for face in range(2):
        for part in range(2):
            small.append(
                pltpu.make_async_copy(
                    inflow_hbm.at[0, face, part],
                    infl.at[face, :, pl.ds(part * 256, 256)],
                    load_sem.at[2 + len(small)],
                )
            )
            small.append(
                pltpu.make_async_copy(
                    robin_hbm.at[0, face, part],
                    rob.at[face, :, pl.ds(part * 512, 512)],
                    load_sem.at[2 + len(small)],
                )
            )
            small.append(
                pltpu.make_async_copy(
                    outflow_hbm.at[0, part, :, pl.ds(face * 512, 512)],
                    outf.at[face, :, pl.ds(part * 512, 512)],
                    load_sem.at[2 + len(small)],
                )
            )
    for copy in small:
        copy.start()

    barrier = pltpu.get_barrier_semaphore()

    @pl.loop(1, n_col)
    def _(k):
        other = lax.rem(col + k, n_col)
        pl.semaphore_signal(barrier, inc=1, device_id=(row, other), device_id_type=MESH)

    for k in range(1, n_row):
        other = lax.rem(row + k, n_row)
        pl.semaphore_signal(barrier, inc=1, device_id=(other, col), device_id_type=MESH)
    for other in (up, down):
        pl.semaphore_signal(
            barrier,
            inc=1,
            device_id=(other // n_col, lax.rem(other, n_col)),
            device_id_type=MESH,
        )
    pl.semaphore_wait(barrier, n_col - 1 + n_row - 1 + 2)
    for copy in loads:
        copy.wait()

    def operate(step):
        sends = []

        def send(index, target, half=None):
            if half is None:
                ref, arrive = vfull.at[index], ag_recv.at[index, 0]
            else:
                ref = vfull.at[index, pl.ds(half * half_rows, half_rows)]
                arrive = ag_recv.at[index, half]
            copy = pltpu.make_async_remote_copy(
                src_ref=ref,
                dst_ref=ref,
                send_sem=ag_send.at[len(sends)],
                recv_sem=arrive,
                device_id=(row, target),
                device_id_type=MESH,
            )
            copy.start()
            sends.append(copy)

        def await_chunk(index, halves):
            if halves:
                for half in range(2):
                    ref = vfull.at[index, pl.ds(half * half_rows, half_rows)]
                    pltpu.make_async_remote_copy(
                        src_ref=ref, dst_ref=ref, send_sem=ag_send.at[0],
                        recv_sem=ag_recv.at[index, half],
                        device_id=(row, partner), device_id_type=MESH,
                    ).wait_recv()
            else:
                ref = vfull.at[index]
                pltpu.make_async_remote_copy(
                    src_ref=ref, dst_ref=ref, send_sem=ag_send.at[0],
                    recv_sem=ag_recv.at[index, 0],
                    device_id=(row, partner), device_id_type=MESH,
                ).wait_recv()

        def multiply(index):
            @pl.when(step == 0)
            def _():
                dense_copy(0, index).wait()
                dense_copy(1, index).wait()

            acc[...] += dot3(dstage[index], stacked(vfull[index]))

        acc[...] = jnp.zeros_like(acc)
        late = None
        for da, db in EVENTS:
            index = mine(da, db)
            if (da, db) != (0, 0):
                await_chunk(index, db == 2 or (da == 2 and db == 0))
            if db == 0:
                if da == 0:
                    send(index, mine(1, 0))
                    send(index, mine(-1, 0))
                elif da == -1:
                    send(index, mine(1, 0), 0)
                elif da == 1:
                    send(index, mine(-1, 0), 1)
                send(index, mine(0, 1))
                send(index, mine(0, -1))
            elif db == -1:
                send(index, mine(0, 1), 0)
            elif db == 1:
                send(index, mine(0, -1), 1)
            send(index, partner)
            if late is None:
                multiply(index)
            else:
                await_chunk(late, False)

                def two(j, carry, index=index, late=late):
                    multiply(index * (1 - j) + late * j)
                    return carry

                lax.fori_loop(0, 2, two, 0)
            late = theirs(da, db)
        await_chunk(late, False)
        multiply(late)
        for copy in sends:
            copy.wait_send()

        @pl.when(step == 0)
        def _():
            gmat[...] = jnp.where(
                tid_ref[...] == lax.broadcasted_iota(jnp.int32, gmat.shape, 1), 1.0, 0.0
            ).astype(jnp.bfloat16)

        def y_copy(k):
            other = lax.rem(row + k, n_row)
            return pltpu.make_async_remote_copy(
                src_ref=gbuf.at[other],
                dst_ref=ybuf.at[row],
                send_sem=y_send.at[k],
                recv_sem=y_recv.at[row],
                device_id=(other, col),
                device_id_type=MESH,
            )

        def y_wait(k):
            other = lax.rem(row + k, n_row)
            pltpu.make_async_remote_copy(
                src_ref=gbuf.at[other],
                dst_ref=ybuf.at[other],
                send_sem=y_send.at[k],
                recv_sem=y_recv.at[other],
                device_id=(other, col),
                device_id_type=MESH,
            ).wait_recv()

        def trace(k, carry):
            ahead = n_row - 1 - k
            other = lax.rem(row + ahead, n_row)
            rows = pl.ds(pl.multiple_of(other * 256, 256), 256)
            gbuf[other] = pick(gmat[rows, :], acc[...])

            @pl.when(k < 3)
            def _():
                y_copy(ahead).start()

            return carry

        lax.fori_loop(0, n_row, trace, 0)

        @pl.when(step == 0)
        def _():
            for copy in small:
                copy.wait()

            def face_maps(face, carry):
                real, imag = infl[face, :, 0:256], infl[face, :, 256:512]
                rin[face, :, 0:256] = dot3(rob[face], jnp.concatenate([real, -imag], axis=0))
                rin[face, :, 256:512] = dot3(rob[face], jnp.concatenate([imag, real], axis=0))

                for tile in range(2):
                    at = tile * 256
                    real = rob[face, :, pl.ds(at, 256)]
                    imag = rob[face, :, pl.ds(512 + at, 256)]
                    orob[face, :, pl.ds(at, 256)] = dot3(
                        outf[face], jnp.concatenate([real, -imag], axis=0)
                    )
                    orob[face, :, pl.ds(512 + at, 256)] = dot3(
                        outf[face], jnp.concatenate([imag, real], axis=0)
                    )
                return carry

            lax.fori_loop(0, 2, face_maps, 0)

        for k in range(1, n_row):
            y_wait(k)
        sbuf[0] = (gbuf[row] + ybuf[lax.rem(row + 1, n_row)]) + (
            ybuf[lax.rem(row + 2, n_row)] + ybuf[lax.rem(row + 3, n_row)]
        )

        def spread(out, into, send_sem, recv_sem):
            def start(k, carry):
                other = lax.rem(col + k, n_col)
                pltpu.make_async_remote_copy(
                    src_ref=out.at[:, pl.ds(pl.multiple_of(other * 8, 8), 8)],
                    dst_ref=into.at[:, pl.ds(pl.multiple_of(col * 8, 8), 8)],
                    send_sem=send_sem.at[other],
                    recv_sem=recv_sem.at[col],
                    device_id=(row, other),
                    device_id_type=MESH,
                ).start()
                return carry

            lax.fori_loop(1, n_col, start, 0)
            own = pl.ds(pl.multiple_of(col * 8, 8), 8)
            into[:, own, :] = out[:, own, :]

        def collect(out, into, send_sem, recv_sem):
            def finish(k, carry):
                other = lax.rem(col + k, n_col)
                block = pl.ds(pl.multiple_of(other * 8, 8), 8)
                copy = pltpu.make_async_remote_copy(
                    src_ref=out.at[:, block],
                    dst_ref=into.at[:, block],
                    send_sem=send_sem.at[other],
                    recv_sem=recv_sem.at[other],
                    device_id=(row, other),
                    device_id_type=MESH,
                )
                copy.wait_recv()
                copy.wait_send()
                return carry

            lax.fori_loop(1, n_col, finish, 0)

        spread(sbuf, slots, c_send, c_recv)
        for k in range(1, n_row):
            y_copy(k).wait_send()

        @pl.when(step == 0)
        def _():
            def own_map(face, carry):
                real, imag = rin[face, :, 0:256], rin[face, :, 256:512]
                town[:, 0:256] += dot3(outf[face], jnp.concatenate([real, -imag], axis=0))
                town[:, 256:512] += dot3(outf[face], jnp.concatenate([imag, real], axis=0))
                return carry

            town[...] = jnp.zeros_like(town)
            lax.fori_loop(0, 2, own_map, 0)

        collect(sbuf, slots, c_send, c_recv)

        def face_copy(face):
            other = up if face == 1 else down
            return pltpu.make_async_remote_copy(
                src_ref=faces.at[face],
                dst_ref=nbuf.at[1 - face],
                send_sem=f_send.at[face],
                recv_sem=f_recv.at[1 - face],
                device_id=(other // n_col, lax.rem(other, n_col)),
                device_id_type=MESH,
            )

        for face in range(2):
            faces[face] = dot3(rin[face], stacked(slots[0]))
            face_copy(face).start()
        cur[...] = dot3(town[...], stacked(slots[0]))
        for face in range(2):
            face_copy(1 - face).wait_recv()
            exists = (device > 0) if face == 0 else (device < total - 1)
            near = jnp.where(exists, nbuf[face], 0.0)
            cur[...] += dot3(orob[face], stacked(near))
        for face in range(2):
            face_copy(face).wait_send()

        def z_copy(k, receive):
            other = lax.rem(row + k, n_row)
            at = other if receive else row
            return pltpu.make_async_remote_copy(
                src_ref=curh.at[:, pl.ds(pl.multiple_of(other * 64, 64), 64)],
                dst_ref=zbuf.at[:, pl.ds(pl.multiple_of(at * 64, 64), 64)],
                send_sem=z_send.at[k],
                recv_sem=z_recv.at[at],
                device_id=(other, col),
                device_id_type=MESH,
            )

        for lane in range(2):
            curh[lane] = cur[:, lane * 128 : lane * 128 + 128]
        for k in (2, 1, 3):
            z_copy(k, False).start()
        own = pl.ds(pl.multiple_of(row * 64, 64), 64)
        zbuf[:, own, :] = curh[:, own, :]
        for k in range(1, n_row):
            z_copy(k, True).wait_recv()
        for source in range(n_row):
            for j in range(2):
                for lane in range(2):
                    zz[lane, pl.ds(source * 2 + j, n_col, stride=8), :] = zbuf[
                        lane, pl.ds(source * 64 + j, n_col, stride=2), :
                    ]
        spread(zz, fin, e_send, e_recv)
        for k in range(1, n_row):
            z_copy(k, False).wait_send()
        onehot = jnp.where(
            sid_ref[...] == lax.broadcasted_iota(jnp.int32, (128, 256), 0), 1.0, 0.0
        ).astype(jnp.bfloat16)
        collect(zz, fin, e_send, e_recv)
        back = pick(onehot, jnp.concatenate([fin[0], fin[1]], axis=1))
        basis[step + 1] = back

        @pl.when(step == 0)
        def _():
            vfull[col] = back * SCALE

    @pl.loop(0, ITERS)
    def _(step):
        operate(step)

    waves = out_ref.shape[1] // 2
    u0, b0, b1 = basis[0], basis[1], basis[2]
    sums = [square_terms(u0, waves), *inner_terms(u0, b0, waves), square_terms(b0, waves)]
    sums += [*inner_terms(u0, b1, waves), *inner_terms(b0, b1, waves), square_terms(b1, waves)]
    gram[...] = jnp.zeros_like(gram)
    for i, line in enumerate(sums):
        gram[pl.ds(i, 1), :] = line[None, :]

    def gy_copy(k, receive):
        other = lax.rem(row + k, n_row)
        at = other if receive else row
        return pltpu.make_async_remote_copy(
            src_ref=gram,
            dst_ref=gy.at[at],
            send_sem=gy_send.at[k],
            recv_sem=gy_recv.at[at],
            device_id=(other, col),
            device_id_type=MESH,
        )

    def gc_copy(k, receive):
        other = lax.rem(col + k, n_col)
        at = other if receive else col
        return pltpu.make_async_remote_copy(
            src_ref=gram2,
            dst_ref=gc.at[at],
            send_sem=gc_send.at[k],
            recv_sem=gc_recv.at[at],
            device_id=(row, other),
            device_id_type=MESH,
        )

    for k in (2, 1, 3):
        gy_copy(k, False).start()
    gy[row] = gram[...]
    for k in range(1, n_row):
        gy_copy(k, True).wait_recv()
    for k in range(1, n_row):
        gy_copy(k, False).wait_send()
    gram2[...] = (gy[0] + gy[1]) + (gy[2] + gy[3])

    @pl.loop(1, n_col)
    def _(k):
        gc_copy(k, False).start()

    gc[col] = gram2[...]

    @pl.loop(1, n_col)
    def _(k):
        gc_copy(k, True).wait_recv()

    gram[...] = jnp.sum(gc[...], axis=0)
    first, second = krylov_coefficients([gram[pl.ds(i, 1), :] for i in range(9)])
    out_ref[...] = scale_vector(basis[0], first, waves) + scale_vector(basis[1], second, waves)

    @pl.loop(1, n_col)
    def _(k):
        gc_copy(k, False).wait_send()


def on_device(
    rhs, dense, inflow, robin, outflow, trace_row, trace_count, current_row, current_count
):
    n_row = lax.axis_size("row")
    n_col = lax.axis_size("col")
    row_at = lax.axis_index("row")
    col_at = lax.axis_index("col")
    device_at = row_at * n_col + col_at
    tpair = trace_row.shape[2]
    tback = current_row.shape[2]

    def live(rows, counts, at):
        own = lax.dynamic_index_in_dim(rows, at, 0, keepdims=False)
        count = lax.dynamic_index_in_dim(counts, at, 0, keepdims=False)
        slot = jnp.arange(rows.shape[2], dtype=jnp.int32)[None, :]
        return jnp.where(slot < count[:, None], own, -1)

    tid = live(trace_row, trace_count, col_at).reshape(-1, 1)
    sid = live(current_row, current_count, device_at)
    sid = sid.reshape(n_row, n_col, tback).transpose(1, 0, 2).reshape(1, -1)
    f32 = jnp.float32
    vmem = pltpu.VMEM
    dma = pltpu.SemaphoreType.DMA
    any_spec = pl.BlockSpec(memory_space=pl.ANY)
    vmem_spec = pl.BlockSpec(memory_space=pltpu.VMEM)
    return pl.pallas_call(
        functools.partial(kernel, n_row, n_col),
        out_shape=jax.ShapeDtypeStruct(rhs.shape, f32),
        in_specs=[any_spec] * 5 + [vmem_spec] * 2,
        out_specs=vmem_spec,
        scratch_shapes=[
            vmem((32, 128, 256), f32),
            vmem((32, 512, 256), f32),
            vmem((512, 256), f32),
            vmem((1024, 512), jnp.bfloat16),
            vmem((4, 256, 256), f32),
            vmem((4, 256, 256), f32),
            vmem((1, 256, 256), f32),
            vmem((1, 256, 256), f32),
            vmem((2, 512, 512), f32),
            vmem((2, 512, 1024), f32),
            vmem((2, 256, 1024), f32),
            vmem((2, 512, 512), f32),
            vmem((2, 256, 1024), f32),
            vmem((256, 512), f32),
            vmem((2, 512, 256), f32),
            vmem((2, 512, 256), f32),
            vmem((256, 256), f32),
            vmem((2, 256, 128), f32),
            vmem((2, 256, 128), f32),
            vmem((2, 256, 128), f32),
            vmem((2, 256, 128), f32),
            vmem((3, 128, 256), f32),
            vmem((16, 128), f32),
            vmem((4, 16, 128), f32),
            vmem((16, 128), f32),
            vmem((32, 16, 128), f32),
            dma((14,)), dma((2, 32)), dma((36,)), dma((32, 2)), dma((4,)), dma((4,)),
            dma((32,)), dma((32,)), dma((2,)), dma((2,)), dma((4,)), dma((4,)),
            dma((32,)), dma((32,)), dma((4,)), dma((4,)), dma((32,)), dma((32,)),
        ],
        compiler_params=pltpu.CompilerParams(
            collective_id=0, has_side_effects=True, vmem_limit_bytes=62 * 1024 * 1024
        ),
        name="gmres",
    )(rhs, dense, inflow, robin, outflow, tid, sid)


def solution(mesh):
    placed = (
        P(("row", "col"), None),
        P(None, "col", "row"),
        P(("row", "col"), None, None, None, None),
        P(("row", "col"), None, None, None, None),
        P(("row", "col"), None, None, None),
        P(),
        P(),
        P(),
        P(),
    )
    return jax.shard_map(
        on_device, mesh=mesh, in_specs=placed, out_specs=P(("row", "col"), None), check_vma=False
    )
```

time: 406 us -> 161 us (0.40); the launches traced: 399 us -> 161 us
  Pallas kernels: 0 us -> 155 us
  waiting for transfers between devices: 129 us -> 0 us
  blocking collectives: 116 us -> 0 us
  matrix products: 58 us -> 0 us
  starting transfers between devices: 33 us -> 0 us
  local copies, waits for them, and re-layouts: 30.6 us -> 5.21 us
  other arithmetic: 18.5 us -> 0.93 us
  between operations: 14.2 us -> 0.04 us
    pallas_call x0 -> x1, Pallas kernels: none -> 155 us  [on_device(): pl.pallas_call(functools.partial(kernel, n_row, n_col), out_shape=jax.Sha...]
    all_gather x2 -> x0, waiting for transfers between devices: 93.3 us -> none  [on_device(): piece = lax.all_gather(operate_vector, 'col', axis=0, tiled=True)]
    psum x1 -> x0, blocking collectives: 63 us -> none  [on_device(): sums = lax.psum(jnp.stack(sums, axis=0), ('row', 'col'))]
    dot_general x12 -> x0, matrix products: 58 us -> none  [the longest x2 19.3 us: on_device(): jnp.dot(real_cols, piece, precision=HIGH, preferred_element_type=jnp.floa...]
    all_to_all x2 -> x0, blocking collectives: 53.2 us -> none  [on_device(): lax.all_to_all(buffer, ('row', 'col'), split_axis=0, concat_axis=0, tiled...]
    all_to_all x2 -> x0, starting transfers between devices: 22.6 us -> none  [on_device(): lax.all_to_all(currents.reshape(devices, tback, lanes), ('row', 'col'), s...]
    all_to_all x2 -> x0, waiting for transfers between devices: 20.8 us -> none  [on_device(): lax.all_to_all(currents.reshape(devices, tback, lanes), ('row', 'col'), s...]
    ppermute x4 -> x0, waiting for transfers between devices: 14 us -> none  [the longest x2 8.79 us: extended(): after = lax.ppermute(leading, axis, down)]
  transfers between devices with their start and end apart: 8 -> 0, of which waited for: 8 -> 0; matrix products, arithmetic and copies ran while one was open for 1% -> 0% of each run, Pallas kernels for 0% -> 0%
where the time goes in v2:
time: 161 us
  Pallas kernels  155 us (96%)
  local copies, waits for them, and re-layouts  5.21 us (3%)
    pallas_call x1, Pallas kernels, on_device(): pl.pallas_call(functools.partial(kernel, n_row, n_col), out_shape=jax.Sha...  155 us

profile of v2, /device:TPU:1, one launch (start us, length us, event | category | flops | bytes accessed | tf_op | source)
XLA Modules:
  0.0 161.1 jit_solution(10454216333316025708)
XLA Ops:
  0.0 0.0 copy-start
  0.0 0.7 constant_dynamic-slice_fusion
  0.7 0.1 squeeze.13
  0.8 0.7 fusion.1
  1.5 0.1 lt.61
  1.6 0.1 copy.15
  1.7 0.7 reshape.50.sid_ref
  2.4 0.0 copy-done
  2.4 0.1 copy.12
  2.5 0.2 squeeze.14
  2.7 0.7 fusion
  3.4 0.1 iota_compare_fusion
  3.5 0.2 lt.64
  3.8 0.8 broadcast_select_fusion.tid_ref
  4.6 155.0 %gmres.1 = f32[128,256]{1,0:T(8,128)} custom-call(f32[128,256]{1,0:T(8,128)} %rhs_hbm.1, f32[2,512,4096]{2,1,0:T(8,128)} %dense_hbm.1, f32[1,2,2,512,256]{4,3,2,1,0:T(8,128)} %inflow_hbm.1, f32[1,2,2,512,512]{4,3,2,1,0:T(8,128)} %robin_hbm.1, f32[1,2,256,1024]{3,2,1,0:T(8,128)} %outflow_hbm.1, s32[1024,1]{1,0:T(8,128)} %broadcast_select_fusion.tid_ref, ...), custom_call_target="tpu_custom_call" | custom-call | tf_op jit(solution)/shard_map/gmres/pallas_call | solution.py:653
  159.6 1.6 copy.17
  (2 shorter events, 0.0 us)
Async XLA Ops:
  0.0 2.4 %copy-start = (s32[32,128,8]{1,2,0:T(8,128)S(1)}, s32[32,128,8]{1,2,0:T(8,128)}, u32[]{:S(2)}) copy-start(s32[32,128,8]{1,2,0:T(8,128)} %param.14) | copy-start | bytes 393220

commit v3 on v2

--- a/solution.py
+++ b/solution.py
@@ -183,19 +183,23 @@
 
 
 EVENTS = [
-    (0, 0), (-1, 0), (1, 0), (0, -1), (0, 1), (2, 0), (-1, -1), (-1, 1),
-    (1, -1), (1, 1), (0, 2), (2, -1), (2, 1), (-1, 2), (1, 2), (2, 2),
+    (-1, 0, 0), (1, 0, 1), (0, -1, 0), (0, 1, 1), (-1, 0, 1), (1, 0, 0), (0, -1, 1), (0, 1, 0),
+    (2, 0, 0), (2, 0, 1), (-1, -1, 0), (1, 1, 1), (1, -1, 1), (-1, 1, 0), (0, 2, 0), (0, 2, 1),
+    (-1, -1, 1), (1, 1, 0), (1, -1, 0), (-1, 1, 1), (-1, 2, 0), (1, 2, 1), (2, -1, 0), (2, 1, 1),
+    (2, -1, 1), (2, 1, 0), (1, 2, 0), (-1, 2, 1), (2, 2, 0), (2, 2, 1),
 ]
 
 
 def kernel(
     n_row, n_col,
-    rhs_hbm, dense_hbm, inflow_hbm, robin_hbm, outflow_hbm, tid_ref, sid_ref,
+    rhs_hbm, dense_hbm, inflow_hbm, robin_hbm, outflow_hbm,
+    trow_hbm, tcount_hbm, crow_hbm, ccount_hbm,
     out_ref,
-    vfull, dstage, acc, gmat, gbuf, ybuf, sbuf, slots, infl, rob, outf,
-    rin, orob, town, faces, nbuf, cur, curh, zbuf, zz, fin, basis, gram, gy, gram2, gc,
+    vfull, dstage, acc, gmat, smat, gbuf, ybuf, rbuf, rsum, sbuf, slots, infl, rob, outf,
+    rin, orob, orecv, town, tmap, faces, nbuf, cur, curh, zbuf, zz, fin, basis, gram, gy, gram2, gc,
+    trow, tcount, crow, ccount,
     load_sem, dsem, ag_send, ag_recv, y_send, y_recv, c_send, c_recv,
-    f_send, f_recv, z_send, z_recv, e_send, e_recv, gy_send, gy_recv, gc_send, gc_recv,
+    o_send, o_recv, f_send, f_recv, z_send, z_recv, e_send, e_recv, gy_send, gy_recv, gc_send, gc_recv,
 ):
     row = lax.axis_index("row")
     col = lax.axis_index("col")
@@ -228,7 +232,13 @@
         pltpu.make_async_copy(rhs_hbm, vfull.at[col], load_sem.at[0]),
         pltpu.make_async_copy(rhs_hbm, basis.at[0], load_sem.at[1]),
     ]
-    for copy in loads:
+    tables = [
+        pltpu.make_async_copy(trow_hbm.at[col], trow, load_sem.at[14]),
+        pltpu.make_async_copy(tcount_hbm, tcount, load_sem.at[15]),
+        pltpu.make_async_copy(crow_hbm.at[device], crow, load_sem.at[16]),
+        pltpu.make_async_copy(ccount_hbm, ccount, load_sem.at[17]),
+    ]
+    for copy in loads + tables:
         copy.start()
 
     def dense_copy(part, index):
@@ -238,37 +248,42 @@
             dsem.at[part, index],
         )
 
-    @pl.loop(0, n_col)
+    inner, outer = [], []
+    for face in range(2):
+        for part in range(2):
+            inner.append(
+                pltpu.make_async_copy(
+                    inflow_hbm.at[0, face, part],
+                    infl.at[face, :, pl.ds(part * 256, 256)],
+                    load_sem.at[2 + len(inner)],
+                )
+            )
+            outer.append(
+                pltpu.make_async_copy(
+                    robin_hbm.at[0, face, part],
+                    rob.at[face, :, pl.ds(part * 512, 512)],
+                    load_sem.at[6 + len(outer)],
+                )
+            )
+            outer.append(
+                pltpu.make_async_copy(
+                    outflow_hbm.at[0, part, :, pl.ds(face * 512, 512)],
+                    outf.at[face, :, pl.ds(part * 512, 512)],
+                    load_sem.at[6 + len(outer)],
+                )
+            )
+    dense_copy(0, col).start()
+    dense_copy(1, col).start()
+    for copy in outer:
+        copy.start()
+
+    @pl.loop(1, n_col)
     def _(k):
         index = lax.rem(col + k, n_col)
         dense_copy(0, index).start()
         dense_copy(1, index).start()
 
-    small = []
-    for face in range(2):
-        for part in range(2):
-            small.append(
-                pltpu.make_async_copy(
-                    inflow_hbm.at[0, face, part],
-                    infl.at[face, :, pl.ds(part * 256, 256)],
-                    load_sem.at[2 + len(small)],
-                )
-            )
-            small.append(
-                pltpu.make_async_copy(
-                    robin_hbm.at[0, face, part],
-                    rob.at[face, :, pl.ds(part * 512, 512)],
-                    load_sem.at[2 + len(small)],
-                )
-            )
-            small.append(
-                pltpu.make_async_copy(
-                    outflow_hbm.at[0, part, :, pl.ds(face * 512, 512)],
-                    outf.at[face, :, pl.ds(part * 512, 512)],
-                    load_sem.at[2 + len(small)],
-                )
-            )
-    for copy in small:
+    for copy in inner:
         copy.start()
 
     barrier = pltpu.get_barrier_semaphore()
@@ -288,46 +303,112 @@
             device_id=(other // n_col, lax.rem(other, n_col)),
             device_id_type=MESH,
         )
+
+    for copy in tables:
+        copy.wait()
+    f32, i32, b16 = jnp.float32, jnp.int32, jnp.bfloat16
+    slot = lax.broadcasted_iota(i32, (8, 128), 0)
+    traced = jnp.where(slot < tcount[pl.ds(col, 1), :], trow[...], -1)
+    traced = jnp.concatenate([traced, jnp.zeros((120, 128), i32)], axis=0)
+    at_row = lax.broadcasted_iota(i32, (1024, 128), 0)
+    at_lane = lax.broadcasted_iota(i32, (1024, 128), 1)
+    expand = jnp.where(at_row // 8 == at_lane, 1.0, 0.0).astype(b16)
+    across = (((1,), (1,)), ((), ()))
+
+    def spread_rows(x):
+        return lax.dot_general(
+            expand, x.astype(f32).astype(b16), across, preferred_element_type=f32
+        )
+
+    table = 16.0 * spread_rows(traced >> 4) + spread_rows(traced & 15)
+    row_id = jnp.sum(jnp.where(at_row % 8 == at_lane, table, 0.0), axis=1, keepdims=True)
+    gmat[...] = jnp.where(
+        row_id.astype(i32) == lax.broadcasted_iota(i32, gmat.shape, 1), 1.0, 0.0
+    ).astype(b16)
+    slot = lax.broadcasted_iota(i32, (2, 128), 0)
+    given = jnp.where(slot < ccount[pl.ds(device, 1), :], crow[...], -1)
+    given = jnp.concatenate([given, jnp.zeros((14, 128), i32)], axis=0)
+    at_row = lax.broadcasted_iota(i32, (128, 256), 0)
+    at_lane = lax.broadcasted_iota(i32, (128, 256), 1)
+    order = jnp.where(at_row == (at_lane // 2 % 4) * 32 + at_lane // 8, 1.0, 0.0).astype(b16)
+    table = mm(given.astype(f32).astype(b16), order)
+    lane = lax.broadcasted_iota(i32, (1, 256), 1)
+    target = jnp.where(lane % 2 == 0, table[0:1, :], table[1:2, :])
+    smat[...] = jnp.where(
+        target.astype(i32) == lax.broadcasted_iota(i32, smat.shape, 0), 1.0, 0.0
+    ).astype(b16)
+
     pl.semaphore_wait(barrier, n_col - 1 + n_row - 1 + 2)
     for copy in loads:
         copy.wait()
 
+    def sign(part):
+        return (2 * part - 1).astype(jnp.float32)
+
+    def outer_map(i, carry):
+        face, tile, part = i // 4, i // 2 % 2, i % 2
+        here = pl.multiple_of(part * 512 + tile * 256, 256)
+        there = pl.multiple_of((1 - part) * 512 + tile * 256, 256)
+        pair = [rob[face, :, pl.ds(here, 256)], rob[face, :, pl.ds(there, 256)] * sign(part)]
+        orob[face, :, pl.ds(here, 256)] = dot3(outf[face], jnp.concatenate(pair, axis=0))
+        return carry
+
+    def halves(ref, face, part):
+        here = ref[face, :, pl.ds(pl.multiple_of(part * 256, 256), 256)]
+        there = ref[face, :, pl.ds(pl.multiple_of((1 - part) * 256, 256), 256)]
+        return jnp.concatenate([here, there * sign(part)], axis=0)
+
+    def inner_map(i, carry):
+        face, part = i // 2, i % 2
+        at = pl.ds(pl.multiple_of(part * 256, 256), 256)
+        rin[face, :, at] = dot3(rob[face], halves(infl, face, part))
+        return carry
+
+    def own_map(part, carry):
+        at = pl.ds(pl.multiple_of(part * 256, 256), 256)
+        town[:, at] = dot3(outf[0], halves(rin, 0, part)) + dot3(outf[1], halves(rin, 1, part))
+        return carry
+
+    def side_map(i, carry):
+        face, part = i // 2, i % 2
+        at = pl.ds(pl.multiple_of(part * 256, 256), 256)
+        tmap[face, :, at] = dot3(orecv[face], halves(rin, face, part))
+        return carry
+
+    def side_copy(source, target, send_sem, recv_sem, face):
+        other = up if face == 1 else down
+        return pltpu.make_async_remote_copy(
+            src_ref=source.at[face],
+            dst_ref=target.at[1 - face],
+            send_sem=send_sem.at[face],
+            recv_sem=recv_sem.at[1 - face],
+            device_id=(other // n_col, lax.rem(other, n_col)),
+            device_id_type=MESH,
+        )
+
     def operate(step):
         sends = []
 
-        def send(index, target, half=None):
-            if half is None:
-                ref, arrive = vfull.at[index], ag_recv.at[index, 0]
-            else:
-                ref = vfull.at[index, pl.ds(half * half_rows, half_rows)]
-                arrive = ag_recv.at[index, half]
+        def send(index, target, half):
+            ref = vfull.at[index, pl.ds(half * half_rows, half_rows)]
             copy = pltpu.make_async_remote_copy(
                 src_ref=ref,
                 dst_ref=ref,
                 send_sem=ag_send.at[len(sends)],
-                recv_sem=arrive,
+                recv_sem=ag_recv.at[index, half],
                 device_id=(row, target),
                 device_id_type=MESH,
             )
             copy.start()
             sends.append(copy)
 
-        def await_chunk(index, halves):
-            if halves:
-                for half in range(2):
-                    ref = vfull.at[index, pl.ds(half * half_rows, half_rows)]
-                    pltpu.make_async_remote_copy(
-                        src_ref=ref, dst_ref=ref, send_sem=ag_send.at[0],
-                        recv_sem=ag_recv.at[index, half],
-                        device_id=(row, partner), device_id_type=MESH,
-                    ).wait_recv()
-            else:
-                ref = vfull.at[index]
-                pltpu.make_async_remote_copy(
-                    src_ref=ref, dst_ref=ref, send_sem=ag_send.at[0],
-                    recv_sem=ag_recv.at[index, 0],
-                    device_id=(row, partner), device_id_type=MESH,
-                ).wait_recv()
+        def await_half(index, half):
+            ref = vfull.at[index, pl.ds(half * half_rows, half_rows)]
+            pltpu.make_async_remote_copy(
+                src_ref=ref, dst_ref=ref, send_sem=ag_send.at[0],
+                recv_sem=ag_recv.at[index, half],
+                device_id=(row, partner), device_id_type=MESH,
+            ).wait_recv()
 
         def multiply(index):
             @pl.when(step == 0)
@@ -338,113 +419,129 @@
             acc[...] += dot3(dstage[index], stacked(vfull[index]))
 
         acc[...] = jnp.zeros_like(acc)
-        late = None
-        for da, db in EVENTS:
+        for half in range(2):
+            send(col, mine(1, 0), half)
+            send(col, mine(-1, 0), 1 - half)
+        for half in range(2):
+            send(col, mine(0, 1), half)
+            send(col, mine(0, -1), 1 - half)
+        for half in range(2):
+            send(col, partner, half)
+        multiply(col)
+
+        @pl.when(step == 0)
+        def _():
+            for copy in outer:
+                copy.wait()
+            lax.fori_loop(0, 3, outer_map, 0)
+
+        ready, seen, done = [(0, 0)], {}, 1
+        for number, (da, db, half) in enumerate(EVENTS):
             index = mine(da, db)
-            if (da, db) != (0, 0):
-                await_chunk(index, db == 2 or (da == 2 and db == 0))
+            await_half(index, half)
             if db == 0:
-                if da == 0:
-                    send(index, mine(1, 0))
-                    send(index, mine(-1, 0))
-                elif da == -1:
-                    send(index, mine(1, 0), 0)
-                elif da == 1:
-                    send(index, mine(-1, 0), 1)
-                send(index, mine(0, 1))
-                send(index, mine(0, -1))
-            elif db == -1:
-                send(index, mine(0, 1), 0)
-            elif db == 1:
-                send(index, mine(0, -1), 1)
-            send(index, partner)
-            if late is None:
-                multiply(index)
-            else:
-                await_chunk(late, False)
-
-                def two(j, carry, index=index, late=late):
-                    multiply(index * (1 - j) + late * j)
-                    return carry
-
-                lax.fori_loop(0, 2, two, 0)
-            late = theirs(da, db)
-        await_chunk(late, False)
+                if da == -1 and half == 0:
+                    send(index, mine(1, 0), half)
+                elif da == 1 and half == 1:
+                    send(index, mine(-1, 0), half)
+                send(index, mine(0, 1), half)
+                send(index, mine(0, -1), half)
+            elif db == -1 and half == 0:
+                send(index, mine(0, 1), half)
+            elif db == 1 and half == 1:
+                send(index, mine(0, -1), half)
+            send(index, partner, half)
+            seen[da, db] = seen.get((da, db), 0) + 1
+            if seen[da, db] == 2:
+                ready.append((da, db))
+            if number == 3:
+
+                @pl.when(step == 0)
+                def _():
+                    lax.fori_loop(3, 6, outer_map, 0)
+
+            if number == 9:
+
+                @pl.when(step == 0)
+                def _():
+                    lax.fori_loop(6, 8, outer_map, 0)
+
+            last = number == len(EVENTS) - 1
+            if number % 2 == 1:
+                for _ in range(len(ready) - done if last else min(2, len(ready) - done)):
+                    index, late = mine(*ready[done]), theirs(*ready[done - 1])
+                    for half in range(2):
+                        await_half(late, half)
+
+                    def two(j, carry, index=index, late=late):
+                        multiply(index * (1 - j) + late * j)
+                        return carry
+
+                    lax.fori_loop(0, 2, two, 0)
+                    done += 1
+        late = theirs(*ready[-1])
+        for half in range(2):
+            await_half(late, half)
         multiply(late)
         for copy in sends:
             copy.wait_send()
 
-        @pl.when(step == 0)
-        def _():
-            gmat[...] = jnp.where(
-                tid_ref[...] == lax.broadcasted_iota(jnp.int32, gmat.shape, 1), 1.0, 0.0
-            ).astype(jnp.bfloat16)
-
-        def y_copy(k):
-            other = lax.rem(row + k, n_row)
+        above, below = lax.rem(row + 1, n_row), lax.rem(row + 3, n_row)
+        low, high = pl.ds(0, 128), pl.ds(128, 128)
+
+        def y_copy(number, source, target, other):
             return pltpu.make_async_remote_copy(
-                src_ref=gbuf.at[other],
-                dst_ref=ybuf.at[row],
-                send_sem=y_send.at[k],
-                recv_sem=y_recv.at[row],
+                src_ref=source,
+                dst_ref=target,
+                send_sem=y_send.at[number],
+                recv_sem=y_recv.at[number],
                 device_id=(other, col),
                 device_id_type=MESH,
             )
 
-        def y_wait(k):
-            other = lax.rem(row + k, n_row)
-            pltpu.make_async_remote_copy(
-                src_ref=gbuf.at[other],
-                dst_ref=ybuf.at[other],
-                send_sem=y_send.at[k],
-                recv_sem=y_recv.at[other],
-                device_id=(other, col),
-                device_id_type=MESH,
-            ).wait_recv()
-
-        def trace(k, carry):
-            ahead = n_row - 1 - k
-            other = lax.rem(row + ahead, n_row)
+        far = lax.rem(row + 2, n_row)
+        y_copies = [
+            y_copy(0, gbuf.at[far, low], rbuf.at[0], above),
+            y_copy(1, gbuf.at[far, high], rbuf.at[1], below),
+            y_copy(2, gbuf.at[above, high], ybuf.at[0, high], above),
+            y_copy(3, gbuf.at[below, low], ybuf.at[1, low], below),
+            y_copy(4, rsum.at[0], ybuf.at[0, low], above),
+            y_copy(5, rsum.at[1], ybuf.at[1, high], below),
+        ]
+
+        @pl.when(step == 0)
+        def _():
+            for face in range(2):
+                side_copy(orob, orecv, o_send, o_recv, face).start()
+
+        def trace(other):
             rows = pl.ds(pl.multiple_of(other * 256, 256), 256)
             gbuf[other] = pick(gmat[rows, :], acc[...])
 
-            @pl.when(k < 3)
-            def _():
-                y_copy(ahead).start()
-
-            return carry
-
-        lax.fori_loop(0, n_row, trace, 0)
+        trace(far)
+        y_copies[0].start()
+        y_copies[1].start()
+        trace(above)
+        y_copies[2].start()
+        trace(below)
+        y_copies[3].start()
+        trace(row)
+        y_copies[0].wait_recv()
+        rsum[0] = gbuf[above, 0:128] + rbuf[0]
+        y_copies[4].start()
+        y_copies[1].wait_recv()
+        rsum[1] = gbuf[below, 128:256] + rbuf[1]
+        y_copies[5].start()
 
         @pl.when(step == 0)
         def _():
-            for copy in small:
+            for copy in inner:
                 copy.wait()
-
-            def face_maps(face, carry):
-                real, imag = infl[face, :, 0:256], infl[face, :, 256:512]
-                rin[face, :, 0:256] = dot3(rob[face], jnp.concatenate([real, -imag], axis=0))
-                rin[face, :, 256:512] = dot3(rob[face], jnp.concatenate([imag, real], axis=0))
-
-                for tile in range(2):
-                    at = tile * 256
-                    real = rob[face, :, pl.ds(at, 256)]
-                    imag = rob[face, :, pl.ds(512 + at, 256)]
-                    orob[face, :, pl.ds(at, 256)] = dot3(
-                        outf[face], jnp.concatenate([real, -imag], axis=0)
-                    )
-                    orob[face, :, pl.ds(512 + at, 256)] = dot3(
-                        outf[face], jnp.concatenate([imag, real], axis=0)
-                    )
-                return carry
-
-            lax.fori_loop(0, 2, face_maps, 0)
-
-        for k in range(1, n_row):
-            y_wait(k)
-        sbuf[0] = (gbuf[row] + ybuf[lax.rem(row + 1, n_row)]) + (
-            ybuf[lax.rem(row + 2, n_row)] + ybuf[lax.rem(row + 3, n_row)]
-        )
+            lax.fori_loop(0, 4, inner_map, 0)
+
+        for copy in y_copies[2:]:
+            copy.wait_recv()
+        sbuf[0] = gbuf[row] + (ybuf[0] + ybuf[1])
 
         def spread(out, into, send_sem, recv_sem):
             def start(k, carry):
@@ -482,44 +579,30 @@
             lax.fori_loop(1, n_col, finish, 0)
 
         spread(sbuf, slots, c_send, c_recv)
-        for k in range(1, n_row):
-            y_copy(k).wait_send()
+        for copy in y_copies:
+            copy.wait_send()
 
         @pl.when(step == 0)
         def _():
-            def own_map(face, carry):
-                real, imag = rin[face, :, 0:256], rin[face, :, 256:512]
-                town[:, 0:256] += dot3(outf[face], jnp.concatenate([real, -imag], axis=0))
-                town[:, 256:512] += dot3(outf[face], jnp.concatenate([imag, real], axis=0))
-                return carry
-
-            town[...] = jnp.zeros_like(town)
             lax.fori_loop(0, 2, own_map, 0)
+            for face in range(2):
+                side_copy(orob, orecv, o_send, o_recv, face).wait_send()
+                side_copy(orob, orecv, o_send, o_recv, 1 - face).wait_recv()
+            lax.fori_loop(0, 4, side_map, 0)
 
         collect(sbuf, slots, c_send, c_recv)
 
-        def face_copy(face):
-            other = up if face == 1 else down
-            return pltpu.make_async_remote_copy(
-                src_ref=faces.at[face],
-                dst_ref=nbuf.at[1 - face],
-                send_sem=f_send.at[face],
-                recv_sem=f_recv.at[1 - face],
-                device_id=(other // n_col, lax.rem(other, n_col)),
-                device_id_type=MESH,
-            )
-
+        ahead = stacked(slots[0])
         for face in range(2):
-            faces[face] = dot3(rin[face], stacked(slots[0]))
-            face_copy(face).start()
-        cur[...] = dot3(town[...], stacked(slots[0]))
+            faces[face] = dot3(tmap[face], ahead)
+            side_copy(faces, nbuf, f_send, f_recv, face).start()
+        cur[...] = dot3(town[...], ahead)
         for face in range(2):
-            face_copy(1 - face).wait_recv()
+            side_copy(faces, nbuf, f_send, f_recv, 1 - face).wait_recv()
             exists = (device > 0) if face == 0 else (device < total - 1)
-            near = jnp.where(exists, nbuf[face], 0.0)
-            cur[...] += dot3(orob[face], stacked(near))
+            cur[...] += jnp.where(exists, nbuf[face], 0.0)
         for face in range(2):
-            face_copy(face).wait_send()
+            side_copy(faces, nbuf, f_send, f_recv, face).wait_send()
 
         def z_copy(k, receive):
             other = lax.rem(row + k, n_row)
@@ -550,11 +633,8 @@
         spread(zz, fin, e_send, e_recv)
         for k in range(1, n_row):
             z_copy(k, False).wait_send()
-        onehot = jnp.where(
-            sid_ref[...] == lax.broadcasted_iota(jnp.int32, (128, 256), 0), 1.0, 0.0
-        ).astype(jnp.bfloat16)
         collect(zz, fin, e_send, e_recv)
-        back = pick(onehot, jnp.concatenate([fin[0], fin[1]], axis=1))
+        back = pick(smat[...], jnp.concatenate([fin[0], fin[1]], axis=1))
         basis[step + 1] = back
 
         @pl.when(step == 0)
@@ -630,21 +710,6 @@
 ):
     n_row = lax.axis_size("row")
     n_col = lax.axis_size("col")
-    row_at = lax.axis_index("row")
-    col_at = lax.axis_index("col")
-    device_at = row_at * n_col + col_at
-    tpair = trace_row.shape[2]
-    tback = current_row.shape[2]
-
-    def live(rows, counts, at):
-        own = lax.dynamic_index_in_dim(rows, at, 0, keepdims=False)
-        count = lax.dynamic_index_in_dim(counts, at, 0, keepdims=False)
-        slot = jnp.arange(rows.shape[2], dtype=jnp.int32)[None, :]
-        return jnp.where(slot < count[:, None], own, -1)
-
-    tid = live(trace_row, trace_count, col_at).reshape(-1, 1)
-    sid = live(current_row, current_count, device_at)
-    sid = sid.reshape(n_row, n_col, tback).transpose(1, 0, 2).reshape(1, -1)
     f32 = jnp.float32
     vmem = pltpu.VMEM
     dma = pltpu.SemaphoreType.DMA
@@ -653,15 +718,18 @@
     return pl.pallas_call(
         functools.partial(kernel, n_row, n_col),
         out_shape=jax.ShapeDtypeStruct(rhs.shape, f32),
-        in_specs=[any_spec] * 5 + [vmem_spec] * 2,
+        in_specs=[any_spec] * 9,
         out_specs=vmem_spec,
         scratch_shapes=[
             vmem((32, 128, 256), f32),
             vmem((32, 512, 256), f32),
             vmem((512, 256), f32),
             vmem((1024, 512), jnp.bfloat16),
+            vmem((128, 256), jnp.bfloat16),
             vmem((4, 256, 256), f32),
-            vmem((4, 256, 256), f32),
+            vmem((2, 256, 256), f32),
+            vmem((2, 128, 256), f32),
+            vmem((2, 128, 256), f32),
             vmem((1, 256, 256), f32),
             vmem((1, 256, 256), f32),
             vmem((2, 512, 512), f32),
@@ -669,9 +737,11 @@
             vmem((2, 256, 1024), f32),
             vmem((2, 512, 512), f32),
             vmem((2, 256, 1024), f32),
+            vmem((2, 256, 1024), f32),
             vmem((256, 512), f32),
-            vmem((2, 512, 256), f32),
-            vmem((2, 512, 256), f32),
+            vmem((2, 256, 512), f32),
+            vmem((2, 256, 256), f32),
+            vmem((2, 256, 256), f32),
             vmem((256, 256), f32),
             vmem((2, 256, 128), f32),
             vmem((2, 256, 128), f32),
@@ -682,15 +752,20 @@
             vmem((4, 16, 128), f32),
             vmem((16, 128), f32),
             vmem((32, 16, 128), f32),
-            dma((14,)), dma((2, 32)), dma((36,)), dma((32, 2)), dma((4,)), dma((4,)),
-            dma((32,)), dma((32,)), dma((2,)), dma((2,)), dma((4,)), dma((4,)),
+            vmem((8, 128), jnp.int32), vmem((32, 128), jnp.int32),
+            vmem((2, 128), jnp.int32), vmem((128, 128), jnp.int32),
+            dma((18,)), dma((2, 32)), dma((62,)), dma((32, 2)), dma((6,)), dma((6,)),
+            dma((32,)), dma((32,)), dma((2,)), dma((2,)), dma((2,)), dma((2,)), dma((4,)), dma((4,)),
             dma((32,)), dma((32,)), dma((4,)), dma((4,)), dma((32,)), dma((32,)),
         ],
         compiler_params=pltpu.CompilerParams(
             collective_id=0, has_side_effects=True, vmem_limit_bytes=62 * 1024 * 1024
         ),
         name="gmres",
-    )(rhs, dense, inflow, robin, outflow, tid, sid)
+    )(
+        rhs, dense, inflow, robin, outflow,
+        trace_row.transpose(0, 2, 1), trace_count, current_row.transpose(0, 2, 1), current_count,
+    )
 
 
 def solution(mesh):

time: 161 us -> 150 us (0.932)
  Pallas kernels: 155 us -> 149 us
  local copies, waits for them, and re-layouts: 5.21 us -> 1.57 us
    pallas_call x1, Pallas kernels: 155 us -> 149 us  [on_device(): pl.pallas_call(functools.partial(kernel, n_row, n_col), out_shape=jax.Sha...]
where the time goes in v3:
time: 150 us
  Pallas kernels  149 us (99%)
  local copies, waits for them, and re-layouts  1.57 us (1%)
    pallas_call x1, Pallas kernels, on_device(): pl.pallas_call(functools.partial(kernel, n_row, n_col), out_shape=jax.Sha...  149 us

profile of v3, /device:TPU:1, one launch (start us, length us, event | category | flops | bytes accessed | tf_op | source)
XLA Modules:
  0.0 150.3 jit_solution(8292108460314806704)
XLA Ops:
  0.0 148.7 %gmres.1 = f32[128,256]{1,0:T(8,128)} custom-call(f32[128,256]{1,0:T(8,128)} %rhs_hbm.1, f32[2,512,4096]{2,1,0:T(8,128)} %dense_hbm.1, f32[1,2,2,512,256]{4,3,2,1,0:T(8,128)} %inflow_hbm.1, f32[1,2,2,512,512]{4,3,2,1,0:T(8,128)} %robin_hbm.1, f32[1,2,256,1024]{3,2,1,0:T(8,128)} %outflow_hbm.1, s32[32,8,128]{2,1,0:T(8,128)} %bitcast.2, s32[32,128]{1,0:T(8,128)} %tcount_hbm.1, ...), custom_call_target="tpu_custom_call" | custom-call | tf_op jit(solution)/shard_map/gmres/pallas_call | solution.py:718
  148.8 1.6 %copy.11 = f32[128,256]{1,0:T(8,128)} copy(f32[128,256]{1,0:T(8,128)} %gmres.1) | data formatting | bytes 262144

commit v4 on v3

--- a/solution.py
+++ b/solution.py
@@ -182,12 +182,24 @@
     return jnp.concatenate([x, turned(x)], axis=0)
 
 
+LAG = 2
 EVENTS = [
     (-1, 0, 0), (1, 0, 1), (0, -1, 0), (0, 1, 1), (-1, 0, 1), (1, 0, 0), (0, -1, 1), (0, 1, 0),
     (2, 0, 0), (2, 0, 1), (-1, -1, 0), (1, 1, 1), (1, -1, 1), (-1, 1, 0), (0, 2, 0), (0, 2, 1),
     (-1, -1, 1), (1, 1, 0), (1, -1, 0), (-1, 1, 1), (-1, 2, 0), (1, 2, 1), (2, -1, 0), (2, 1, 1),
     (2, -1, 1), (2, 1, 0), (1, 2, 0), (-1, 2, 1), (2, 2, 0), (2, 2, 1),
 ]
+
+
+READY = [(0, 0)]
+for _i, _event in enumerate(EVENTS):
+    if _event[:2] in [_e[:2] for _e in EVENTS[:_i]]:
+        READY.append(_event[:2])
+
+OFFSETS = sorted(
+    [(dz, dx, dk) for dz in range(4) for dx in range(4) for dk in range(2)],
+    key=lambda o: -(min(o[0], 4 - o[0]) + min(o[1], 4 - o[1]) + 0.1 * o[2]),
+)[:-1]
 
 
 def kernel(
@@ -226,6 +238,10 @@
         )
 
     partner = col + 1 - 2 * core
+
+    def offset_col(dz, dx, dk):
+        return lax.rem(z + dz, 4) * 8 + lax.rem(x + dx, 4) * 2 + lax.rem(core + dk, 2)
+
     half_rows = vfull.shape[1] // 2
 
     loads = [
@@ -277,14 +293,14 @@
     for copy in outer:
         copy.start()
 
-    @pl.loop(1, n_col)
-    def _(k):
-        index = lax.rem(col + k, n_col)
-        dense_copy(0, index).start()
-        dense_copy(1, index).start()
-
-    for copy in inner:
-        copy.start()
+    for number, spot in enumerate(READY):
+        for index in ([] if number == 0 else [mine(*spot)]) + [theirs(*spot)]:
+            dense_copy(0, index).start()
+            dense_copy(1, index).start()
+        if number == 6:
+            for copy in inner:
+                copy.start()
+
 
     barrier = pltpu.get_barrier_semaphore()
 
@@ -359,9 +375,9 @@
         return jnp.concatenate([here, there * sign(part)], axis=0)
 
     def inner_map(i, carry):
-        face, part = i // 2, i % 2
+        face, part, rows = i // 4, i // 2 % 2, pl.ds(pl.multiple_of(i % 2 * 256, 256), 256)
         at = pl.ds(pl.multiple_of(part * 256, 256), 256)
-        rin[face, :, at] = dot3(rob[face], halves(infl, face, part))
+        rin[face, rows, at] = dot3(rob[face, rows, :], halves(infl, face, part))
         return carry
 
     def own_map(part, carry):
@@ -385,6 +401,54 @@
             device_id=(other // n_col, lax.rem(other, n_col)),
             device_id_type=MESH,
         )
+
+    waves = out_ref.shape[1] // 2
+
+    def gy_copy(part, k, receive):
+        other = lax.rem(row + k, n_row)
+        at = other if receive else row
+        return pltpu.make_async_remote_copy(
+            src_ref=gram.at[part],
+            dst_ref=gy.at[part, at],
+            send_sem=gy_send.at[part, k],
+            recv_sem=gy_recv.at[part, at],
+            device_id=(other, col),
+            device_id_type=MESH,
+        )
+
+    def gc_copy(part, offset, receive):
+        other = offset_col(*offset)
+        at = other if receive else col
+        return pltpu.make_async_remote_copy(
+            src_ref=gram2.at[part],
+            dst_ref=gc.at[part, at],
+            send_sem=gc_send.at[part, other],
+            recv_sem=gc_recv.at[part, at],
+            device_id=(row, other),
+            device_id_type=MESH,
+        )
+
+    def over_row(part, lines):
+        gram[part] = jnp.zeros((8, waves), jnp.float32)
+        for i, line in enumerate(lines):
+            gram[part, pl.ds(i, 1), :] = line[None, :]
+        for k in (2, 1, 3):
+            gy_copy(part, k, False).start()
+        gy[part, row] = gram[part]
+
+    def over_col(part):
+        for k in range(1, n_row):
+            gy_copy(part, k, True).wait_recv()
+        for k in range(1, n_row):
+            gy_copy(part, k, False).wait_send()
+        gram2[part] = (gy[part, 0] + gy[part, 1]) + (gy[part, 2] + gy[part, 3])
+        for offset in OFFSETS:
+            gc_copy(part, offset, False).start()
+        gc[part, col] = gram2[part]
+
+    def finish_col(part):
+        for offset in OFFSETS:
+            gc_copy(part, offset, True).wait_recv()
 
     def operate(step):
         sends = []
@@ -427,6 +491,12 @@
             send(col, mine(0, -1), 1 - half)
         for half in range(2):
             send(col, partner, half)
+        @pl.when(step == 1)
+        def _():
+            u0, b0 = basis[0], basis[1]
+            lines = [square_terms(u0, waves), *inner_terms(u0, b0, waves), square_terms(b0, waves)]
+            over_row(0, lines)
+
         multiply(col)
 
         @pl.when(step == 0)
@@ -454,22 +524,27 @@
             seen[da, db] = seen.get((da, db), 0) + 1
             if seen[da, db] == 2:
                 ready.append((da, db))
-            if number == 3:
+            work = {2: (outer_map, 3, 5), 3: (outer_map, 5, 6), 7: (outer_map, 6, 8)}
+            work.update({9 + 2 * i: (inner_map, i, i + 1) for i in range(8)})
+            if number in work:
 
                 @pl.when(step == 0)
-                def _():
-                    lax.fori_loop(3, 6, outer_map, 0)
-
-            if number == 9:
-
-                @pl.when(step == 0)
-                def _():
-                    lax.fori_loop(6, 8, outer_map, 0)
+                def _(number=number):
+                    if number == 9:
+                        for copy in inner:
+                            copy.wait()
+                    fn, start, stop = work[number]
+                    lax.fori_loop(start, stop, fn, 0)
 
             last = number == len(EVENTS) - 1
             if number % 2 == 1:
                 for _ in range(len(ready) - done if last else min(2, len(ready) - done)):
-                    index, late = mine(*ready[done]), theirs(*ready[done - 1])
+                    index = mine(*ready[done])
+                    if done < LAG:
+                        multiply(index)
+                        done += 1
+                        continue
+                    late = theirs(*ready[done - LAG])
                     for half in range(2):
                         await_half(late, half)
 
@@ -479,12 +554,11 @@
 
                     lax.fori_loop(0, 2, two, 0)
                     done += 1
-        late = theirs(*ready[-1])
-        for half in range(2):
-            await_half(late, half)
-        multiply(late)
-        for copy in sends:
-            copy.wait_send()
+        for spot in ready[-LAG:]:
+            late = theirs(*spot)
+            for half in range(2):
+                await_half(late, half)
+            multiply(late)
 
         above, below = lax.rem(row + 1, n_row), lax.rem(row + 3, n_row)
         low, high = pl.ds(0, 128), pl.ds(128, 128)
@@ -535,17 +609,19 @@
 
         @pl.when(step == 0)
         def _():
-            for copy in inner:
-                copy.wait()
-            lax.fori_loop(0, 4, inner_map, 0)
+            lax.fori_loop(0, 2, own_map, 0)
+
+        @pl.when(step == 1)
+        def _():
+            over_col(0)
 
         for copy in y_copies[2:]:
             copy.wait_recv()
         sbuf[0] = gbuf[row] + (ybuf[0] + ybuf[1])
 
         def spread(out, into, send_sem, recv_sem):
-            def start(k, carry):
-                other = lax.rem(col + k, n_col)
+            for offset in OFFSETS:
+                other = offset_col(*offset)
                 pltpu.make_async_remote_copy(
                     src_ref=out.at[:, pl.ds(pl.multiple_of(other * 8, 8), 8)],
                     dst_ref=into.at[:, pl.ds(pl.multiple_of(col * 8, 8), 8)],
@@ -554,9 +630,6 @@
                     device_id=(row, other),
                     device_id_type=MESH,
                 ).start()
-                return carry
-
-            lax.fori_loop(1, n_col, start, 0)
             own = pl.ds(pl.multiple_of(col * 8, 8), 8)
             into[:, own, :] = out[:, own, :]
 
@@ -579,12 +652,11 @@
             lax.fori_loop(1, n_col, finish, 0)
 
         spread(sbuf, slots, c_send, c_recv)
-        for copy in y_copies:
+        for copy in sends + y_copies:
             copy.wait_send()
 
         @pl.when(step == 0)
         def _():
-            lax.fori_loop(0, 2, own_map, 0)
             for face in range(2):
                 side_copy(orob, orecv, o_send, o_recv, face).wait_send()
                 side_copy(orob, orecv, o_send, o_recv, 1 - face).wait_recv()
@@ -645,64 +717,19 @@
     def _(step):
         operate(step)
 
-    waves = out_ref.shape[1] // 2
     u0, b0, b1 = basis[0], basis[1], basis[2]
-    sums = [square_terms(u0, waves), *inner_terms(u0, b0, waves), square_terms(b0, waves)]
-    sums += [*inner_terms(u0, b1, waves), *inner_terms(b0, b1, waves), square_terms(b1, waves)]
-    gram[...] = jnp.zeros_like(gram)
-    for i, line in enumerate(sums):
-        gram[pl.ds(i, 1), :] = line[None, :]
-
-    def gy_copy(k, receive):
-        other = lax.rem(row + k, n_row)
-        at = other if receive else row
-        return pltpu.make_async_remote_copy(
-            src_ref=gram,
-            dst_ref=gy.at[at],
-            send_sem=gy_send.at[k],
-            recv_sem=gy_recv.at[at],
-            device_id=(other, col),
-            device_id_type=MESH,
-        )
-
-    def gc_copy(k, receive):
-        other = lax.rem(col + k, n_col)
-        at = other if receive else col
-        return pltpu.make_async_remote_copy(
-            src_ref=gram2,
-            dst_ref=gc.at[at],
-            send_sem=gc_send.at[k],
-            recv_sem=gc_recv.at[at],
-            device_id=(row, other),
-            device_id_type=MESH,
-        )
-
-    for k in (2, 1, 3):
-        gy_copy(k, False).start()
-    gy[row] = gram[...]
-    for k in range(1, n_row):
-        gy_copy(k, True).wait_recv()
-    for k in range(1, n_row):
-        gy_copy(k, False).wait_send()
-    gram2[...] = (gy[0] + gy[1]) + (gy[2] + gy[3])
-
-    @pl.loop(1, n_col)
-    def _(k):
-        gc_copy(k, False).start()
-
-    gc[col] = gram2[...]
-
-    @pl.loop(1, n_col)
-    def _(k):
-        gc_copy(k, True).wait_recv()
-
-    gram[...] = jnp.sum(gc[...], axis=0)
-    first, second = krylov_coefficients([gram[pl.ds(i, 1), :] for i in range(9)])
+    over_row(1, [*inner_terms(u0, b1, waves), *inner_terms(b0, b1, waves), square_terms(b1, waves)])
+    over_col(1)
+    finish_col(0)
+    finish_col(1)
+    early, late = jnp.sum(gc[0], axis=0), jnp.sum(gc[1], axis=0)
+    first, second = krylov_coefficients(
+        [early[i : i + 1] for i in range(4)] + [late[i : i + 1] for i in range(5)]
+    )
     out_ref[...] = scale_vector(basis[0], first, waves) + scale_vector(basis[1], second, waves)
-
-    @pl.loop(1, n_col)
-    def _(k):
-        gc_copy(k, False).wait_send()
+    for part in range(2):
+        for offset in OFFSETS:
+            gc_copy(part, offset, False).wait_send()
 
 
 def on_device(
@@ -748,15 +775,15 @@
             vmem((2, 256, 128), f32),
             vmem((2, 256, 128), f32),
             vmem((3, 128, 256), f32),
-            vmem((16, 128), f32),
-            vmem((4, 16, 128), f32),
-            vmem((16, 128), f32),
-            vmem((32, 16, 128), f32),
+            vmem((2, 8, 128), f32),
+            vmem((2, 4, 8, 128), f32),
+            vmem((2, 8, 128), f32),
+            vmem((2, 32, 8, 128), f32),
             vmem((8, 128), jnp.int32), vmem((32, 128), jnp.int32),
             vmem((2, 128), jnp.int32), vmem((128, 128), jnp.int32),
             dma((18,)), dma((2, 32)), dma((62,)), dma((32, 2)), dma((6,)), dma((6,)),
             dma((32,)), dma((32,)), dma((2,)), dma((2,)), dma((2,)), dma((2,)), dma((4,)), dma((4,)),
-            dma((32,)), dma((32,)), dma((4,)), dma((4,)), dma((32,)), dma((32,)),
+            dma((32,)), dma((32,)), dma((2, 4)), dma((2, 4)), dma((2, 32)), dma((2, 32)),
         ],
         compiler_params=pltpu.CompilerParams(
             collective_id=0, has_side_effects=True, vmem_limit_bytes=62 * 1024 * 1024

time: 150 us -> 153 us (1.020)
  Pallas kernels: 149 us -> 151 us
    pallas_call x1, Pallas kernels: 149 us -> 151 us  [on_device(): pl.pallas_call(functools.partial(kernel, n_row, n_col), out_shape=jax.Sha...]
where the time goes in v4:
time: 153 us; the launch traced here: 152 us
  Pallas kernels  151 us (99%)
  local copies, waits for them, and re-layouts  1.57 us (1%)
    pallas_call x1, Pallas kernels, on_device(): pl.pallas_call(functools.partial(kernel, n_row, n_col), out_shape=jax.Sha...  151 us

profile of v4, /device:TPU:1, one launch (start us, length us, event | category | flops | bytes accessed | tf_op | source)
XLA Modules:
  0.0 152.5 jit_solution(7539375442063524685)
XLA Ops:
  0.0 150.9 %gmres.1 = f32[128,256]{1,0:T(8,128)} custom-call(f32[128,256]{1,0:T(8,128)} %rhs_hbm.1, f32[2,512,4096]{2,1,0:T(8,128)} %dense_hbm.1, f32[1,2,2,512,256]{4,3,2,1,0:T(8,128)} %inflow_hbm.1, f32[1,2,2,512,512]{4,3,2,1,0:T(8,128)} %robin_hbm.1, f32[1,2,256,1024]{3,2,1,0:T(8,128)} %outflow_hbm.1, s32[32,8,128]{2,1,0:T(8,128)} %bitcast.2, s32[32,128]{1,0:T(8,128)} %tcount_hbm.1, ...), custom_call_target="tpu_custom_call" | custom-call | tf_op jit(solution)/shard_map/gmres/pallas_call | solution.py:745
  150.9 1.6 %copy.11 = f32[128,256]{1,0:T(8,128)} copy(f32[128,256]{1,0:T(8,128)} %gmres.1) | data formatting | bytes 262144
